TPU v7x, 512 devices: a whole 4x4x16 slice. The times are simulated.
512 devices in a mesh: ctx: 64 (over y, z), head: 8 (over x, core).
Axes of the slice: x: 4, y: 4, z: 16, core: 2. Of those that a mesh axis runs over, the one named last changes fastest.
Arguments:
- query_rows: bfloat16 [32768, 2048], P('ctx', 'head'), parts along dimension 1, may hold values from -6 to 6
- key_rows: bfloat16 [32768, 2048], P('ctx', 'head'), parts along dimension 1, may hold values from -6 to 6
- value_rows: bfloat16 [32768, 2048], P('ctx', 'head'), parts along dimension 1, may hold values from -6 to 6
- out_grad: bfloat16 [32768, 2048], P('ctx', 'head'), parts along dimension 1, may hold values from -6 to 6
- doc_lengths: int32 [64], P('head'), parts along dimension 0, may hold values from 1 to 8192, 32768 in all
Outputs:
- attended: bfloat16 [32768, 2048], P('ctx', 'head'), parts along dimension 1
- grad_query: bfloat16 [32768, 2048], P('ctx', 'head'), parts along dimension 1
- grad_key: bfloat16 [32768, 2048], P('ctx', 'head'), parts along dimension 1
- grad_value: bfloat16 [32768, 2048], P('ctx', 'head'), parts along dimension 1
There are 8 independent parts, one for each index of `head`. A program takes and returns all parts, laid end to end along the dimension named above; each array names one. Nothing has to cross between parts.
Inputs may be any that keep to these rules, and one draw needn't show every extreme that they name: `doc_lengths`: the lengths add up to 32768; the longest document holds exactly 8192 tokens.
All inputs are finite; a program needn't handle non-finite values.
Results may differ from a plain program's by a relative error of at most 0.0051.
Values sent between devices are 32-bit elements; how exact they have to be, the bound alone decides.
A program may use at most 64 MiB of HBM per device.

v0:
```python
import jax
import jax.numpy as jnp
from jax import lax
from jax.sharding import PartitionSpec as P

HD = 128


def shifted(value, axis, steps):
    count = lax.axis_size(axis)
    initial, last = (max(0, -steps), min(count, count - steps))
    return lax.ppermute(value, axis, [(source, source + steps) for source in range(initial, last)])


def doc_layout(doc_lengths, base, rows):
    count = doc_lengths.shape[0]
    starts = jnp.cumsum(doc_lengths) - doc_lengths
    finish = starts + doc_lengths
    positions = base + jnp.arange(rows, dtype=jnp.int32)
    member = (
        (positions[:, None] >= starts[None, :]) & (positions[:, None] < finish[None, :])
    ).astype(jnp.int32)
    labels = jnp.arange(count, dtype=jnp.int32)
    doc_index = jnp.sum(member * labels[None, :], axis=1)
    offsets = positions - jnp.sum(member * starts[None, :], axis=1)
    first_doc = doc_index[0]
    last_doc = doc_index[rows - 1]
    first_start = jnp.sum(jnp.where(labels == first_doc, starts, 0))
    last_start = jnp.sum(jnp.where(labels == last_doc, starts, 0))
    first_finish = jnp.sum(jnp.where(labels == first_doc, finish, 0))
    last_finish = jnp.sum(jnp.where(labels == last_doc, finish, 0))
    carry_in = (first_start < base).astype(jnp.float32)
    reset_fwd = (last_start >= base).astype(jnp.float32)
    reset_bwd = (first_finish <= base + rows).astype(jnp.float32)
    carry_back = (last_finish > base + rows).astype(jnp.float32)
    local = jnp.arange(rows, dtype=jnp.int32)
    allowed = (doc_index[:, None] == doc_index[None, :]) & (local[:, None] >= local[None, :])
    return (
        offsets,
        doc_index == first_doc,
        doc_index == last_doc,
        carry_in,
        reset_fwd,
        reset_bwd,
        carry_back,
        allowed,
    )


def body(query_rows, key_rows, value_rows, out_grad, doc_lengths):
    hi = lax.Precision.HIGHEST
    rows = query_rows.shape[0]
    head_dim = HD
    heads = query_rows.shape[1] // head_dim
    base = lax.axis_index("ctx") * rows
    layout = doc_layout(doc_lengths, base, rows)
    offsets, first_rows, last_rows, carry_in, reset_fwd, reset_bwd, carry_back, allowed = layout
    row_scale = lax.rsqrt(offsets.astype(jnp.float32) + 1.0) * head_dim ** (-0.5)
    query_heads = query_rows.reshape(rows, heads, head_dim)
    key_heads = key_rows.reshape(rows, heads, head_dim)
    value_heads = value_rows.reshape(rows, heads, head_dim)
    grad_heads = out_grad.reshape(rows, heads, head_dim)
    scaled = (query_heads.astype(jnp.float32) * row_scale[:, None, None]).astype(jnp.bfloat16)
    tail_keys = jnp.where(last_rows[:, None, None], key_heads, jnp.zeros_like(key_heads))
    tail_state = jnp.einsum(
        "thd,the->hde", tail_keys, value_heads, preferred_element_type=jnp.float32
    )
    head_queries = jnp.where(first_rows[:, None, None], scaled, jnp.zeros_like(scaled))
    head_state = jnp.einsum(
        "thd,the->hde", head_queries, grad_heads, preferred_element_type=jnp.float32
    )
    zero_state = jnp.zeros((heads, head_dim, head_dim), jnp.float32)
    reach = lax.axis_size("ctx") // 4

    def pass_forward(step_no, carry):
        received = shifted(carry[0], "ctx", 1)
        return (tail_state + (1.0 - reset_fwd) * received, received)

    def pass_backward(step_no, carry):
        received = shifted(carry[0], "ctx", -1)
        return (head_state + (1.0 - reset_bwd) * received, received)

    fwd_carry = lax.fori_loop(0, reach, pass_forward, (tail_state, zero_state))
    bwd_carry = lax.fori_loop(0, reach, pass_backward, (head_state, zero_state))
    entering = fwd_carry[1] * carry_in
    returning = bwd_carry[1] * carry_back
    mask_heads = allowed[None, :, :]
    scores = jnp.einsum("thd,shd->hts", scaled, key_heads, preferred_element_type=jnp.float32)
    weights = jnp.where(mask_heads, scores, 0.0).astype(jnp.bfloat16)
    dscores = jnp.einsum(
        "the,she->hts", grad_heads, value_heads, preferred_element_type=jnp.float32
    )
    dweights = jnp.where(mask_heads, dscores, 0.0).astype(jnp.bfloat16)
    attended = jnp.einsum("thd,hde->the", scaled.astype(jnp.float32), entering, precision=hi)
    attended = attended + jnp.einsum(
        "hts,she->the", weights, value_heads, preferred_element_type=jnp.float32
    )
    grad_q = jnp.einsum("the,hde->thd", grad_heads.astype(jnp.float32), entering, precision=hi)
    grad_q = row_scale[:, None, None] * (
        grad_q + jnp.einsum("hts,shd->thd", dweights, key_heads, preferred_element_type=jnp.float32)
    )
    grad_k = jnp.einsum("she,hde->shd", value_heads.astype(jnp.float32), returning, precision=hi)
    grad_k = grad_k + jnp.einsum(
        "hts,thd->shd", dweights, scaled, preferred_element_type=jnp.float32
    )
    grad_v = jnp.einsum("shd,hde->she", key_heads.astype(jnp.float32), returning, precision=hi)
    grad_v = grad_v + jnp.einsum(
        "hts,the->she", weights, grad_heads, preferred_element_type=jnp.float32
    )
    flat = (rows, heads * head_dim)
    return (
        attended.astype(jnp.bfloat16).reshape(flat),
        grad_q.astype(jnp.bfloat16).reshape(flat),
        grad_k.astype(jnp.bfloat16).reshape(flat),
        grad_v.astype(jnp.bfloat16).reshape(flat),
    )


def solution(mesh):
    in_specs = (P("ctx", "head"), P("ctx", "head"), P("ctx", "head"), P("ctx", "head"), P("head"))
    out_specs = (P("ctx", "head"), P("ctx", "head"), P("ctx", "head"), P("ctx", "head"))
    return jax.shard_map(body, mesh=mesh, in_specs=in_specs, out_specs=out_specs, check_vma=False)
```

profile of v0, /device:TPU:30, one launch (start us, length us, event | category | flops | bytes accessed | tf_op | source)
XLA Modules:
  0.0 339.2 jit_solution(10609272674658190833)
XLA Ops:
  9.1 161.2 %while.29 = (s32[]{:T(128)}, f32[2,128,128]{2,1,0:T(8,128)S(1)}, f32[2,128,128]{2,1,0:T(8,128)}, f32[]{:T(128)}, f32[2,128,128]{2,1,0:T(8,128)S(1)}, /*index=5*/s32[]{:T(128)}) while((s32[]{:T(128)}, f32[2,128,128]{2,1,0:T(8,128)S(1)}, f32[2,128,128]{2,1,0:T(8,128)}, f32[]{:T(128)}, f32[2,128,128]{2,1,0:T(8,128)S(1)}, ...), condition=%wide.region_9.10_spmd, body=%wide.region_8.9_spmd.sunk | while | flops 65538 | bytes 1441933 | solution.py:84
  9.1 11.7 %collective-permute-start.1 = (f32[2,128,128]{2,1,0:T(8,128)S(1)}, f32[2,128,128]{2,1,0:T(8,128)S(1)}, u32[]{:S(2)}, u32[]{:S(2)}) collective-permute-start(f32[2,128,128]{2,1,0:T(8,128)S(1)} %get-tuple-element.245), channel_id=1, source_target_pairs={{8,0},{16,8},{24,16},{32,24},{40,32},{48,40},{56,48},{64,56},{72,6... | collective-permute-start | bytes 393224 | tf_op jit(solution)/shard_map/while/body/eval_jaxpr/ppermute | solution.py:12
  24.2 6.5 %collective-permute-start.1 = (f32[2,128,128]{2,1,0:T(8,128)S(1)}, f32[2,128,128]{2,1,0:T(8,128)S(1)}, u32[]{:S(2)}, u32[]{:S(2)}) collective-permute-start(f32[2,128,128]{2,1,0:T(8,128)S(1)} %get-tuple-element.245), channel_id=1, source_target_pairs={{8,0},{16,8},{24,16},{32,24},{40,32},{48,40},{56,48},{64,56},{72,6... | collective-permute-start | bytes 393224 | tf_op jit(solution)/shard_map/while/body/eval_jaxpr/ppermute | solution.py:12
  43.5 6.5 %collective-permute-start.1 = (f32[2,128,128]{2,1,0:T(8,128)S(1)}, f32[2,128,128]{2,1,0:T(8,128)S(1)}, u32[]{:S(2)}, u32[]{:S(2)}) collective-permute-start(f32[2,128,128]{2,1,0:T(8,128)S(1)} %get-tuple-element.245), channel_id=1, source_target_pairs={{8,0},{16,8},{24,16},{32,24},{40,32},{48,40},{56,48},{64,56},{72,6... | collective-permute-start | bytes 393224 | tf_op jit(solution)/shard_map/while/body/eval_jaxpr/ppermute | solution.py:12
  82.7 6.5 %collective-permute-start.1 = (f32[2,128,128]{2,1,0:T(8,128)S(1)}, f32[2,128,128]{2,1,0:T(8,128)S(1)}, u32[]{:S(2)}, u32[]{:S(2)}) collective-permute-start(f32[2,128,128]{2,1,0:T(8,128)S(1)} %get-tuple-element.245), channel_id=1, source_target_pairs={{8,0},{16,8},{24,16},{32,24},{40,32},{48,40},{56,48},{64,56},{72,6... | collective-permute-start | bytes 393224 | tf_op jit(solution)/shard_map/while/body/eval_jaxpr/ppermute | solution.py:12
  93.2 6.5 %collective-permute-start.1 = (f32[2,128,128]{2,1,0:T(8,128)S(1)}, f32[2,128,128]{2,1,0:T(8,128)S(1)}, u32[]{:S(2)}, u32[]{:S(2)}) collective-permute-start(f32[2,128,128]{2,1,0:T(8,128)S(1)} %get-tuple-element.245), channel_id=1, source_target_pairs={{8,0},{16,8},{24,16},{32,24},{40,32},{48,40},{56,48},{64,56},{72,6... | collective-permute-start | bytes 393224 | tf_op jit(solution)/shard_map/while/body/eval_jaxpr/ppermute | solution.py:12
  103.0 6.5 %collective-permute-start.1 = (f32[2,128,128]{2,1,0:T(8,128)S(1)}, f32[2,128,128]{2,1,0:T(8,128)S(1)}, u32[]{:S(2)}, u32[]{:S(2)}) collective-permute-start(f32[2,128,128]{2,1,0:T(8,128)S(1)} %get-tuple-element.245), channel_id=1, source_target_pairs={{8,0},{16,8},{24,16},{32,24},{40,32},{48,40},{56,48},{64,56},{72,6... | collective-permute-start | bytes 393224 | tf_op jit(solution)/shard_map/while/body/eval_jaxpr/ppermute | solution.py:12
  177.9 156.2 %while.28 = (s32[]{:T(128)}, f32[2,128,128]{2,1,0:T(8,128)S(1)}, f32[2,128,128]{2,1,0:T(8,128)}, f32[]{:T(128)}, f32[2,128,128]{2,1,0:T(8,128)S(1)}, /*index=5*/s32[]{:T(128)}) while((s32[]{:T(128)}, f32[2,128,128]{2,1,0:T(8,128)S(1)}, f32[2,128,128]{2,1,0:T(8,128)}, f32[]{:T(128)}, f32[2,128,128]{2,1,0:T(8,128)S(1)}, ...), condition=%wide.region_4.5_spmd, body=%wide.region_3.4_spmd.sunk | while | flops 65538 | bytes 1441933 | solution.py:83
  179.8 7.5 %collective-permute-done = f32[2,128,128]{2,1,0:T(8,128)S(1)} collective-permute-done((f32[2,128,128]{2,1,0:T(8,128)S(1)}, f32[2,128,128]{2,1,0:T(8,128)S(1)}, u32[]{:S(2)}, u32[]{:S(2)}) %collective-permute-start) | collective-permute-done | bytes 131104 | tf_op jit(solution)/shard_map/while/body/eval_jaxpr/ppermute | solution.py:12
  189.9 7.0 %collective-permute-done = f32[2,128,128]{2,1,0:T(8,128)S(1)} collective-permute-done((f32[2,128,128]{2,1,0:T(8,128)S(1)}, f32[2,128,128]{2,1,0:T(8,128)S(1)}, u32[]{:S(2)}, u32[]{:S(2)}) %collective-permute-start) | collective-permute-done | bytes 131104 | tf_op jit(solution)/shard_map/while/body/eval_jaxpr/ppermute | solution.py:12
  199.5 7.0 %collective-permute-done = f32[2,128,128]{2,1,0:T(8,128)S(1)} collective-permute-done((f32[2,128,128]{2,1,0:T(8,128)S(1)}, f32[2,128,128]{2,1,0:T(8,128)S(1)}, u32[]{:S(2)}, u32[]{:S(2)}) %collective-permute-start) | collective-permute-done | bytes 131104 | tf_op jit(solution)/shard_map/while/body/eval_jaxpr/ppermute | solution.py:12
  209.1 7.0 %collective-permute-done = f32[2,128,128]{2,1,0:T(8,128)S(1)} collective-permute-done((f32[2,128,128]{2,1,0:T(8,128)S(1)}, f32[2,128,128]{2,1,0:T(8,128)S(1)}, u32[]{:S(2)}, u32[]{:S(2)}) %collective-permute-start) | collective-permute-done | bytes 131104 | tf_op jit(solution)/shard_map/while/body/eval_jaxpr/ppermute | solution.py:12
  218.7 7.0 %collective-permute-done = f32[2,128,128]{2,1,0:T(8,128)S(1)} collective-permute-done((f32[2,128,128]{2,1,0:T(8,128)S(1)}, f32[2,128,128]{2,1,0:T(8,128)S(1)}, u32[]{:S(2)}, u32[]{:S(2)}) %collective-permute-start) | collective-permute-done | bytes 131104 | tf_op jit(solution)/shard_map/while/body/eval_jaxpr/ppermute | solution.py:12
  228.4 7.1 %collective-permute-done = f32[2,128,128]{2,1,0:T(8,128)S(1)} collective-permute-done((f32[2,128,128]{2,1,0:T(8,128)S(1)}, f32[2,128,128]{2,1,0:T(8,128)S(1)}, u32[]{:S(2)}, u32[]{:S(2)}) %collective-permute-start) | collective-permute-done | bytes 131104 | tf_op jit(solution)/shard_map/while/body/eval_jaxpr/ppermute | solution.py:12
  238.1 8.3 %collective-permute-done = f32[2,128,128]{2,1,0:T(8,128)S(1)} collective-permute-done((f32[2,128,128]{2,1,0:T(8,128)S(1)}, f32[2,128,128]{2,1,0:T(8,128)S(1)}, u32[]{:S(2)}, u32[]{:S(2)}) %collective-permute-start) | collective-permute-done | bytes 131104 | tf_op jit(solution)/shard_map/while/body/eval_jaxpr/ppermute | solution.py:12
  248.9 7.6 %collective-permute-done = f32[2,128,128]{2,1,0:T(8,128)S(1)} collective-permute-done((f32[2,128,128]{2,1,0:T(8,128)S(1)}, f32[2,128,128]{2,1,0:T(8,128)S(1)}, u32[]{:S(2)}, u32[]{:S(2)}) %collective-permute-start) | collective-permute-done | bytes 131104 | tf_op jit(solution)/shard_map/while/body/eval_jaxpr/ppermute | solution.py:12
  259.1 7.0 %collective-permute-done = f32[2,128,128]{2,1,0:T(8,128)S(1)} collective-permute-done((f32[2,128,128]{2,1,0:T(8,128)S(1)}, f32[2,128,128]{2,1,0:T(8,128)S(1)}, u32[]{:S(2)}, u32[]{:S(2)}) %collective-permute-start) | collective-permute-done | bytes 131104 | tf_op jit(solution)/shard_map/while/body/eval_jaxpr/ppermute | solution.py:12
  268.7 7.0 %collective-permute-done = f32[2,128,128]{2,1,0:T(8,128)S(1)} collective-permute-done((f32[2,128,128]{2,1,0:T(8,128)S(1)}, f32[2,128,128]{2,1,0:T(8,128)S(1)}, u32[]{:S(2)}, u32[]{:S(2)}) %collective-permute-start) | collective-permute-done | bytes 131104 | tf_op jit(solution)/shard_map/while/body/eval_jaxpr/ppermute | solution.py:12
  278.3 7.0 %collective-permute-done = f32[2,128,128]{2,1,0:T(8,128)S(1)} collective-permute-done((f32[2,128,128]{2,1,0:T(8,128)S(1)}, f32[2,128,128]{2,1,0:T(8,128)S(1)}, u32[]{:S(2)}, u32[]{:S(2)}) %collective-permute-start) | collective-permute-done | bytes 131104 | tf_op jit(solution)/shard_map/while/body/eval_jaxpr/ppermute | solution.py:12
  288.0 7.0 %collective-permute-done = f32[2,128,128]{2,1,0:T(8,128)S(1)} collective-permute-done((f32[2,128,128]{2,1,0:T(8,128)S(1)}, f32[2,128,128]{2,1,0:T(8,128)S(1)}, u32[]{:S(2)}, u32[]{:S(2)}) %collective-permute-start) | collective-permute-done | bytes 131104 | tf_op jit(solution)/shard_map/while/body/eval_jaxpr/ppermute | solution.py:12
  297.6 7.0 %collective-permute-done = f32[2,128,128]{2,1,0:T(8,128)S(1)} collective-permute-done((f32[2,128,128]{2,1,0:T(8,128)S(1)}, f32[2,128,128]{2,1,0:T(8,128)S(1)}, u32[]{:S(2)}, u32[]{:S(2)}) %collective-permute-start) | collective-permute-done | bytes 131104 | tf_op jit(solution)/shard_map/while/body/eval_jaxpr/ppermute | solution.py:12
  307.2 7.0 %collective-permute-done = f32[2,128,128]{2,1,0:T(8,128)S(1)} collective-permute-done((f32[2,128,128]{2,1,0:T(8,128)S(1)}, f32[2,128,128]{2,1,0:T(8,128)S(1)}, u32[]{:S(2)}, u32[]{:S(2)}) %collective-permute-start) | collective-permute-done | bytes 131104 | tf_op jit(solution)/shard_map/while/body/eval_jaxpr/ppermute | solution.py:12
  316.8 7.0 %collective-permute-done = f32[2,128,128]{2,1,0:T(8,128)S(1)} collective-permute-done((f32[2,128,128]{2,1,0:T(8,128)S(1)}, f32[2,128,128]{2,1,0:T(8,128)S(1)}, u32[]{:S(2)}, u32[]{:S(2)}) %collective-permute-start) | collective-permute-done | bytes 131104 | tf_op jit(solution)/shard_map/while/body/eval_jaxpr/ppermute | solution.py:12
  326.4 7.0 %collective-permute-done = f32[2,128,128]{2,1,0:T(8,128)S(1)} collective-permute-done((f32[2,128,128]{2,1,0:T(8,128)S(1)}, f32[2,128,128]{2,1,0:T(8,128)S(1)}, u32[]{:S(2)}, u32[]{:S(2)}) %collective-permute-start) | collective-permute-done | bytes 131104 | tf_op jit(solution)/shard_map/while/body/eval_jaxpr/ppermute | solution.py:12
  (181 shorter events, 176.2 us)
Async XLA Ops:
  9.1 14.4 %collective-permute-start.1 = (f32[2,128,128]{2,1,0:T(8,128)S(1)}, f32[2,128,128]{2,1,0:T(8,128)S(1)}, u32[]{:S(2)}, u32[]{:S(2)}) collective-permute-start(f32[2,128,128]{2,1,0:T(8,128)S(1)} %get-tuple-element.245), channel_id=1, source_target_pairs={{8,0},{16,8},{24,16},{32,24},{40,32},{48,40},{56,48},{64,56},{72,6... | collective-permute-start | bytes 393224 | tf_op jit(solution)/shard_map/while/body/eval_jaxpr/ppermute | solution.py:12
  24.2 9.0 %collective-permute-start.1 = (f32[2,128,128]{2,1,0:T(8,128)S(1)}, f32[2,128,128]{2,1,0:T(8,128)S(1)}, u32[]{:S(2)}, u32[]{:S(2)}) collective-permute-start(f32[2,128,128]{2,1,0:T(8,128)S(1)} %get-tuple-element.245), channel_id=1, source_target_pairs={{8,0},{16,8},{24,16},{32,24},{40,32},{48,40},{56,48},{64,56},{72,6... | collective-permute-start | bytes 393224 | tf_op jit(solution)/shard_map/while/body/eval_jaxpr/ppermute | solution.py:12
  33.9 9.0 %collective-permute-start.1 = (f32[2,128,128]{2,1,0:T(8,128)S(1)}, f32[2,128,128]{2,1,0:T(8,128)S(1)}, u32[]{:S(2)}, u32[]{:S(2)}) collective-permute-start(f32[2,128,128]{2,1,0:T(8,128)S(1)} %get-tuple-element.245), channel_id=1, source_target_pairs={{8,0},{16,8},{24,16},{32,24},{40,32},{48,40},{56,48},{64,56},{72,6... | collective-permute-start | bytes 393224 | tf_op jit(solution)/shard_map/while/body/eval_jaxpr/ppermute | solution.py:12
  43.5 9.0 %collective-permute-start.1 = (f32[2,128,128]{2,1,0:T(8,128)S(1)}, f32[2,128,128]{2,1,0:T(8,128)S(1)}, u32[]{:S(2)}, u32[]{:S(2)}) collective-permute-start(f32[2,128,128]{2,1,0:T(8,128)S(1)} %get-tuple-element.245), channel_id=1, source_target_pairs={{8,0},{16,8},{24,16},{32,24},{40,32},{48,40},{56,48},{64,56},{72,6... | collective-permute-start | bytes 393224 | tf_op jit(solution)/shard_map/while/body/eval_jaxpr/ppermute | solution.py:12
  53.1 9.0 %collective-permute-start.1 = (f32[2,128,128]{2,1,0:T(8,128)S(1)}, f32[2,128,128]{2,1,0:T(8,128)S(1)}, u32[]{:S(2)}, u32[]{:S(2)}) collective-permute-start(f32[2,128,128]{2,1,0:T(8,128)S(1)} %get-tuple-element.245), channel_id=1, source_target_pairs={{8,0},{16,8},{24,16},{32,24},{40,32},{48,40},{56,48},{64,56},{72,6... | collective-permute-start | bytes 393224 | tf_op jit(solution)/shard_map/while/body/eval_jaxpr/ppermute | solution.py:12
  62.7 9.0 %collective-permute-start.1 = (f32[2,128,128]{2,1,0:T(8,128)S(1)}, f32[2,128,128]{2,1,0:T(8,128)S(1)}, u32[]{:S(2)}, u32[]{:S(2)}) collective-permute-start(f32[2,128,128]{2,1,0:T(8,128)S(1)} %get-tuple-element.245), channel_id=1, source_target_pairs={{8,0},{16,8},{24,16},{32,24},{40,32},{48,40},{56,48},{64,56},{72,6... | collective-permute-start | bytes 393224 | tf_op jit(solution)/shard_map/while/body/eval_jaxpr/ppermute | solution.py:12
  72.4 9.7 %collective-permute-start.1 = (f32[2,128,128]{2,1,0:T(8,128)S(1)}, f32[2,128,128]{2,1,0:T(8,128)S(1)}, u32[]{:S(2)}, u32[]{:S(2)}) collective-permute-start(f32[2,128,128]{2,1,0:T(8,128)S(1)} %get-tuple-element.245), channel_id=1, source_target_pairs={{8,0},{16,8},{24,16},{32,24},{40,32},{48,40},{56,48},{64,56},{72,6... | collective-permute-start | bytes 393224 | tf_op jit(solution)/shard_map/while/body/eval_jaxpr/ppermute | solution.py:12
  82.7 9.9 %collective-permute-start.1 = (f32[2,128,128]{2,1,0:T(8,128)S(1)}, f32[2,128,128]{2,1,0:T(8,128)S(1)}, u32[]{:S(2)}, u32[]{:S(2)}) collective-permute-start(f32[2,128,128]{2,1,0:T(8,128)S(1)} %get-tuple-element.245), channel_id=1, source_target_pairs={{8,0},{16,8},{24,16},{32,24},{40,32},{48,40},{56,48},{64,56},{72,6... | collective-permute-start | bytes 393224 | tf_op jit(solution)/shard_map/while/body/eval_jaxpr/ppermute | solution.py:12
  93.2 9.1 %collective-permute-start.1 = (f32[2,128,128]{2,1,0:T(8,128)S(1)}, f32[2,128,128]{2,1,0:T(8,128)S(1)}, u32[]{:S(2)}, u32[]{:S(2)}) collective-permute-start(f32[2,128,128]{2,1,0:T(8,128)S(1)} %get-tuple-element.245), channel_id=1, source_target_pairs={{8,0},{16,8},{24,16},{32,24},{40,32},{48,40},{56,48},{64,56},{72,6... | collective-permute-start | bytes 393224 | tf_op jit(solution)/shard_map/while/body/eval_jaxpr/ppermute | solution.py:12
  103.0 9.0 %collective-permute-start.1 = (f32[2,128,128]{2,1,0:T(8,128)S(1)}, f32[2,128,128]{2,1,0:T(8,128)S(1)}, u32[]{:S(2)}, u32[]{:S(2)}) collective-permute-start(f32[2,128,128]{2,1,0:T(8,128)S(1)} %get-tuple-element.245), channel_id=1, source_target_pairs={{8,0},{16,8},{24,16},{32,24},{40,32},{48,40},{56,48},{64,56},{72,6... | collective-permute-start | bytes 393224 | tf_op jit(solution)/shard_map/while/body/eval_jaxpr/ppermute | solution.py:12
  112.6 9.0 %collective-permute-start.1 = (f32[2,128,128]{2,1,0:T(8,128)S(1)}, f32[2,128,128]{2,1,0:T(8,128)S(1)}, u32[]{:S(2)}, u32[]{:S(2)}) collective-permute-start(f32[2,128,128]{2,1,0:T(8,128)S(1)} %get-tuple-element.245), channel_id=1, source_target_pairs={{8,0},{16,8},{24,16},{32,24},{40,32},{48,40},{56,48},{64,56},{72,6... | collective-permute-start | bytes 393224 | tf_op jit(solution)/shard_map/while/body/eval_jaxpr/ppermute | solution.py:12
  122.2 9.0 %collective-permute-start.1 = (f32[2,128,128]{2,1,0:T(8,128)S(1)}, f32[2,128,128]{2,1,0:T(8,128)S(1)}, u32[]{:S(2)}, u32[]{:S(2)}) collective-permute-start(f32[2,128,128]{2,1,0:T(8,128)S(1)} %get-tuple-element.245), channel_id=1, source_target_pairs={{8,0},{16,8},{24,16},{32,24},{40,32},{48,40},{56,48},{64,56},{72,6... | collective-permute-start | bytes 393224 | tf_op jit(solution)/shard_map/while/body/eval_jaxpr/ppermute | solution.py:12
  131.8 9.0 %collective-permute-start.1 = (f32[2,128,128]{2,1,0:T(8,128)S(1)}, f32[2,128,128]{2,1,0:T(8,128)S(1)}, u32[]{:S(2)}, u32[]{:S(2)}) collective-permute-start(f32[2,128,128]{2,1,0:T(8,128)S(1)} %get-tuple-element.245), channel_id=1, source_target_pairs={{8,0},{16,8},{24,16},{32,24},{40,32},{48,40},{56,48},{64,56},{72,6... | collective-permute-start | bytes 393224 | tf_op jit(solution)/shard_map/while/body/eval_jaxpr/ppermute | solution.py:12
  141.5 9.0 %collective-permute-start.1 = (f32[2,128,128]{2,1,0:T(8,128)S(1)}, f32[2,128,128]{2,1,0:T(8,128)S(1)}, u32[]{:S(2)}, u32[]{:S(2)}) collective-permute-start(f32[2,128,128]{2,1,0:T(8,128)S(1)} %get-tuple-element.245), channel_id=1, source_target_pairs={{8,0},{16,8},{24,16},{32,24},{40,32},{48,40},{56,48},{64,56},{72,6... | collective-permute-start | bytes 393224 | tf_op jit(solution)/shard_map/while/body/eval_jaxpr/ppermute | solution.py:12
  151.1 9.0 %collective-permute-start.1 = (f32[2,128,128]{2,1,0:T(8,128)S(1)}, f32[2,128,128]{2,1,0:T(8,128)S(1)}, u32[]{:S(2)}, u32[]{:S(2)}) collective-permute-start(f32[2,128,128]{2,1,0:T(8,128)S(1)} %get-tuple-element.245), channel_id=1, source_target_pairs={{8,0},{16,8},{24,16},{32,24},{40,32},{48,40},{56,48},{64,56},{72,6... | collective-permute-start | bytes 393224 | tf_op jit(solution)/shard_map/while/body/eval_jaxpr/ppermute | solution.py:12
  160.7 9.0 %collective-permute-start.1 = (f32[2,128,128]{2,1,0:T(8,128)S(1)}, f32[2,128,128]{2,1,0:T(8,128)S(1)}, u32[]{:S(2)}, u32[]{:S(2)}) collective-permute-start(f32[2,128,128]{2,1,0:T(8,128)S(1)} %get-tuple-element.245), channel_id=1, source_target_pairs={{8,0},{16,8},{24,16},{32,24},{40,32},{48,40},{56,48},{64,56},{72,6... | collective-permute-start | bytes 393224 | tf_op jit(solution)/shard_map/while/body/eval_jaxpr/ppermute | solution.py:12
  177.9 9.4 %collective-permute-start = (f32[2,128,128]{2,1,0:T(8,128)S(1)}, f32[2,128,128]{2,1,0:T(8,128)S(1)}, u32[]{:S(2)}, u32[]{:S(2)}) collective-permute-start(f32[2,128,128]{2,1,0:T(8,128)S(1)} %get-tuple-element.227), channel_id=1, source_target_pairs={{0,8},{8,16},{16,24},{24,32},{32,40},{40,48},{48,56},{56,64},{64,7... | collective-permute-start | bytes 393224 | tf_op jit(solution)/shard_map/while/body/eval_jaxpr/ppermute | solution.py:12
  188.0 9.0 %collective-permute-start = (f32[2,128,128]{2,1,0:T(8,128)S(1)}, f32[2,128,128]{2,1,0:T(8,128)S(1)}, u32[]{:S(2)}, u32[]{:S(2)}) collective-permute-start(f32[2,128,128]{2,1,0:T(8,128)S(1)} %get-tuple-element.227), channel_id=1, source_target_pairs={{0,8},{8,16},{16,24},{24,32},{32,40},{40,48},{48,56},{56,64},{64,7... | collective-permute-start | bytes 393224 | tf_op jit(solution)/shard_map/while/body/eval_jaxpr/ppermute | solution.py:12
  226.4 9.1 %collective-permute-start = (f32[2,128,128]{2,1,0:T(8,128)S(1)}, f32[2,128,128]{2,1,0:T(8,128)S(1)}, u32[]{:S(2)}, u32[]{:S(2)}) collective-permute-start(f32[2,128,128]{2,1,0:T(8,128)S(1)} %get-tuple-element.227), channel_id=1, source_target_pairs={{0,8},{8,16},{16,24},{24,32},{32,40},{40,48},{48,56},{56,64},{64,7... | collective-permute-start | bytes 393224 | tf_op jit(solution)/shard_map/while/body/eval_jaxpr/ppermute | solution.py:12
  236.2 10.2 %collective-permute-start = (f32[2,128,128]{2,1,0:T(8,128)S(1)}, f32[2,128,128]{2,1,0:T(8,128)S(1)}, u32[]{:S(2)}, u32[]{:S(2)}) collective-permute-start(f32[2,128,128]{2,1,0:T(8,128)S(1)} %get-tuple-element.227), channel_id=1, source_target_pairs={{0,8},{8,16},{16,24},{24,32},{32,40},{40,48},{48,56},{56,64},{64,7... | collective-permute-start | bytes 393224 | tf_op jit(solution)/shard_map/while/body/eval_jaxpr/ppermute | solution.py:12
  247.0 9.5 %collective-permute-start = (f32[2,128,128]{2,1,0:T(8,128)S(1)}, f32[2,128,128]{2,1,0:T(8,128)S(1)}, u32[]{:S(2)}, u32[]{:S(2)}) collective-permute-start(f32[2,128,128]{2,1,0:T(8,128)S(1)} %get-tuple-element.227), channel_id=1, source_target_pairs={{0,8},{8,16},{16,24},{24,32},{32,40},{40,48},{48,56},{56,64},{64,7... | collective-permute-start | bytes 393224 | tf_op jit(solution)/shard_map/while/body/eval_jaxpr/ppermute | solution.py:12
  266.8 9.0 %collective-permute-start = (f32[2,128,128]{2,1,0:T(8,128)S(1)}, f32[2,128,128]{2,1,0:T(8,128)S(1)}, u32[]{:S(2)}, u32[]{:S(2)}) collective-permute-start(f32[2,128,128]{2,1,0:T(8,128)S(1)} %get-tuple-element.227), channel_id=1, source_target_pairs={{0,8},{8,16},{16,24},{24,32},{32,40},{40,48},{48,56},{56,64},{64,7... | collective-permute-start | bytes 393224 | tf_op jit(solution)/shard_map/while/body/eval_jaxpr/ppermute | solution.py:12
  276.4 9.0 %collective-permute-start = (f32[2,128,128]{2,1,0:T(8,128)S(1)}, f32[2,128,128]{2,1,0:T(8,128)S(1)}, u32[]{:S(2)}, u32[]{:S(2)}) collective-permute-start(f32[2,128,128]{2,1,0:T(8,128)S(1)} %get-tuple-element.227), channel_id=1, source_target_pairs={{0,8},{8,16},{16,24},{24,32},{32,40},{40,48},{48,56},{56,64},{64,7... | collective-permute-start | bytes 393224 | tf_op jit(solution)/shard_map/while/body/eval_jaxpr/ppermute | solution.py:12
  324.5 9.0 %collective-permute-start = (f32[2,128,128]{2,1,0:T(8,128)S(1)}, f32[2,128,128]{2,1,0:T(8,128)S(1)}, u32[]{:S(2)}, u32[]{:S(2)}) collective-permute-start(f32[2,128,128]{2,1,0:T(8,128)S(1)} %get-tuple-element.227), channel_id=1, source_target_pairs={{0,8},{8,16},{16,24},{24,32},{32,40},{40,48},{48,56},{56,64},{64,7... | collective-permute-start | bytes 393224 | tf_op jit(solution)/shard_map/while/body/eval_jaxpr/ppermute | solution.py:12
  (45 other events, 435.4 us)
where the time goes:
time: 342 us; the launch traced here: 339 us
  waiting for transfers between devices  157 us (46%)
  starting transfers between devices  139 us (41%)
  local copies, waits for them, and re-layouts  27 us (8%)
  matrix products  6.48 us (2%)
  other arithmetic  5.75 us (2%)
    ppermute x32, waiting for transfers between devices, shifted(): lax.ppermute(value, axis, [(source, source + steps) for source in range(i...  157 us
    ppermute x32, starting transfers between devices, shifted(): lax.ppermute(value, axis, [(source, source + steps) for source in range(i...  139 us
    while x64, local copies, waits for them, and re-layouts  20.3 us
  transfers between devices with their start and end apart: 32, of which 32 were waited for; matrix products, arithmetic and copies ran while one was open for 0% of the time, Pallas kernels for 0%

commit v1 on v0

v1 whole, which is shorter than its diff:
```python
import functools

import jax
import jax.numpy as jnp
from jax import lax
from jax.experimental import pallas as pl
from jax.experimental.pallas import tpu as pltpu
from jax.sharding import PartitionSpec as P

HD = 128
HEADS = 2
ROWS = 512
DOCS = 8
BLOCKS = 64
GROUP = 4
GROUPS = BLOCKS // GROUP
REACH = 4
PIECES = 4
PROWS = HEADS * HD // PIECES
MESH = pl.DeviceIdType.MESH
F32 = jnp.float32
BF16 = jnp.bfloat16
TN = (((0,), (0,)), ((), ()))
NT = (((1,), (1,)), ((), ()))
NN = (((1,), (0,)), ((), ()))


def dot(a, b, dims):
    return lax.dot_general(a, b, dims, preferred_element_type=F32)


def flag(cond):
    return jnp.where(cond, jnp.float32(1.0), jnp.float32(0.0))


def owner(group, piece):
    turned = (group % 4) // 2
    return piece + turned * (3 - 2 * piece)


def split(x):
    hi = x.astype(BF16)
    return hi, (x - hi.astype(F32)).astype(BF16)


def kernel(
    dl_ref, q_ref, k_ref, v_ref, g_ref, att_ref, gq_ref, gk_ref, gv_ref,
    state, near_in, far_out, far_in, back_out, back_in, scaled_s, acc,
    ss1, rs1, ss2, rs2, ss3, rs3,
):
    c = lax.axis_index("ctx")
    h = lax.axis_index("head")
    grp = c // GROUP
    me = c % GROUP
    piece = owner(grp, me)

    def member(i):
        return (grp * GROUP + i, h)

    def far(step):
        other = (grp + step + GROUPS) % GROUPS
        return (other * GROUP + owner(other, piece), h)

    barrier = pltpu.get_barrier_semaphore()
    partners = [member((me + d) % GROUP) for d in range(1, GROUP)]
    partners += [far(s * d) for d in range(1, REACH + 1) for s in (1, -1)]
    for p in partners:
        pl.semaphore_signal(barrier, inc=1, device_id=p, device_id_type=MESH)

    starts, ends = [], []
    total = jnp.int32(0)
    for d in range(DOCS):
        starts.append(total)
        total = total + dl_ref[d]
        ends.append(total)

    def start_of(pos):
        best = jnp.int32(0)
        for d in range(1, DOCS):
            best = jnp.where(starts[d] <= pos, starts[d], best)
        return best

    def end_of(pos):
        best = ends[DOCS - 1]
        for d in range(DOCS - 2, -1, -1):
            best = jnp.where(ends[d] > pos, ends[d], best)
        return best

    base = c * ROWS
    last_start = start_of(base + ROWS - 1)
    first_end = end_of(base)
    pos = base + lax.broadcasted_iota(jnp.int32, (ROWS, HD), 0)
    doc_start = jnp.zeros((ROWS, HD), jnp.int32)
    for d in range(1, DOCS):
        doc_start = jnp.where(pos >= starts[d], starts[d], doc_start)
    row_scale = lax.rsqrt((pos - doc_start).astype(F32) + 1.0) * HD ** (-0.5)
    in_last = pos >= last_start
    in_first = pos < first_end

    for hd in range(HEADS):
        cols = slice(hd * HD, (hd + 1) * HD)
        tail = jnp.where(in_last, k_ref[:, cols].astype(F32), 0.0).astype(BF16)
        st = dot(tail, v_ref[:, cols], TN)
        state[2 * hd, 0] = st[:PROWS]
        state[2 * hd + 1, 0] = st[PROWS:]
        sc = q_ref[:, cols].astype(F32) * row_scale
        scaled_s[:, cols] = sc.astype(BF16)
        head = jnp.where(in_first, sc, 0.0).astype(BF16)
        st = dot(head, g_ref[:, cols], TN)
        state[2 * hd, 1] = st[:PROWS]
        state[2 * hd + 1, 1] = st[PROWS:]

    pl.semaphore_wait(barrier, len(partners))

    def near_copy(i, slot):
        return pltpu.make_async_remote_copy(
            state.at[owner(grp, i)], near_in.at[slot], ss1.at[i], rs1.at[slot],
            device_id=member(i), device_id_type=MESH)

    for d in range(1, GROUP):
        near_copy((me + d) % GROUP, me).start()
    near_in[me] = state[piece]

    def local_work(hd):
        cols = slice(hd * HD, (hd + 1) * HD)
        half = ROWS // 2
        for tb in range(2):
            rows = slice(tb * half, (tb + 1) * half)
            width = (tb + 1) * half
            sc, gr = scaled_s[rows, cols], g_ref[rows, cols]
            ke, va = k_ref[:width, cols], v_ref[:width, cols]
            col = base + lax.broadcasted_iota(jnp.int32, (half, width), 1)
            row = base + tb * half + lax.broadcasted_iota(jnp.int32, (half, width), 0)
            first = jnp.tile(doc_start[rows], (1, width // HD))
            allowed = (col <= row) & (col >= first)
            w = jnp.where(allowed, dot(sc, ke, NT), 0.0).astype(BF16)
            dw = jnp.where(allowed, dot(gr, va, NT), 0.0).astype(BF16)
            acc[0, rows, cols] = dot(w, va, NN)
            acc[1, rows, cols] = dot(dw, ke, NN)
            gk, gv = dot(dw, sc, TN), dot(w, gr, TN)
            if tb == 0:
                acc[2, rows, cols] = gk
                acc[3, rows, cols] = gv
            else:
                acc[2, :half, cols] += gk[:half]
                acc[3, :half, cols] += gv[:half]
                acc[2, half:, cols] = gk[half:]
                acc[3, half:, cols] = gv[half:]

    local_work(0)

    for d in range(1, GROUP):
        i = (me + d) % GROUP
        near_copy(i, i).wait_recv()

    block0 = grp * GROUP
    gbase = block0 * ROWS
    glast_start = start_of(gbase + GROUP * ROWS - 1)
    gfirst_end = end_of(gbase)
    tail_total = near_in[GROUP - 1, 0]
    head_total = near_in[0, 1]
    for i in range(GROUP - 1):
        tail_total += flag(glast_start < gbase + (i + 1) * ROWS) * near_in[i, 0]
        head_total += flag(gfirst_end > gbase + (i + 1) * ROWS) * near_in[i + 1, 1]
    far_out[0] = tail_total
    far_out[1] = head_total

    def far_copy(scan, d):
        return pltpu.make_async_remote_copy(
            far_out.at[scan], far_in.at[scan, d - 1], ss2.at[scan, d - 1], rs2.at[scan, d - 1],
            device_id=far(d if scan == 0 else -d), device_id_type=MESH)

    for d in (2, 3, 1, 4):
        for scan in range(2):
            far_copy(scan, d).start()

    local_work(1)

    for d in range(1, REACH + 1):
        for scan in range(2):
            far_copy(scan, d).wait_recv()

    gfirst_start = start_of(gbase)
    glast_end = end_of(gbase + GROUP * ROWS - 1)
    from_left = flag(gfirst_start < gbase) * far_in[0, 0]
    from_right = flag(glast_end > gbase + GROUP * ROWS) * far_in[1, 0]
    for d in range(2, REACH + 1):
        from_left += flag(gfirst_start < gbase - (d - 1) * GROUP * ROWS) * far_in[0, d - 1]
        from_right += flag(glast_end > gbase + d * GROUP * ROWS) * far_in[1, d - 1]
    for i in range(GROUP):
        at = gbase + i * ROWS
        begin = start_of(at)
        finish = end_of(at + ROWS - 1)
        entering = flag(begin < gbase) * from_left
        for r in range(i):
            entering += flag(begin < gbase + (r + 1) * ROWS) * near_in[r, 0]
        returning = flag(finish > gbase + GROUP * ROWS) * from_right
        for r in range(i + 1, GROUP):
            returning += flag(finish > gbase + r * ROWS) * near_in[r, 1]
        back_out[i, 0] = entering
        back_out[i, 1] = returning

    def back_copy(i, slot):
        return pltpu.make_async_remote_copy(
            back_out.at[i], back_in.at[slot], ss3.at[i], rs3.at[slot],
            device_id=member(i), device_id_type=MESH)

    for d in range(1, GROUP):
        back_copy((me + d) % GROUP, piece).start()
    back_in[piece] = back_out[me]
    for d in range(1, GROUP):
        i = (me + d) % GROUP
        back_copy(i, owner(grp, i)).wait_recv()

    for hd in range(HEADS):
        cols = slice(hd * HD, (hd + 1) * HD)
        e_hi, e_lo = split(jnp.concatenate([back_in[2 * hd, 0], back_in[2 * hd + 1, 0]], axis=0))
        r_hi, r_lo = split(jnp.concatenate([back_in[2 * hd, 1], back_in[2 * hd + 1, 1]], axis=0))
        sc, gr, ke, va = scaled_s[:, cols], g_ref[:, cols], k_ref[:, cols], v_ref[:, cols]
        att = acc[0, :, cols] + dot(sc, e_hi, NN) + dot(sc, e_lo, NN)
        att_ref[:, cols] = att.astype(BF16)
        gq = acc[1, :, cols] + dot(gr, e_hi, NT) + dot(gr, e_lo, NT)
        gq_ref[:, cols] = (row_scale * gq).astype(BF16)
        gk = acc[2, :, cols] + dot(va, r_hi, NT) + dot(va, r_lo, NT)
        gk_ref[:, cols] = gk.astype(BF16)
        gv = acc[3, :, cols] + dot(ke, r_hi, NN) + dot(ke, r_lo, NN)
        gv_ref[:, cols] = gv.astype(BF16)

    for d in range(1, GROUP):
        i = (me + d) % GROUP
        near_copy(i, i).wait_send()
        back_copy(i, i).wait_send()
    for d in range(1, REACH + 1):
        for scan in range(2):
            far_copy(scan, d).wait_send()


def body(query_rows, key_rows, value_rows, out_grad, doc_lengths):
    vmem = pl.BlockSpec(memory_space=pltpu.VMEM)
    out = jax.ShapeDtypeStruct((ROWS, HEADS * HD), BF16)
    dma = pltpu.SemaphoreType.DMA
    return pl.pallas_call(
        kernel,
        out_shape=(out,) * 4,
        in_specs=[pl.BlockSpec(memory_space=pltpu.SMEM)] + [vmem] * 4,
        out_specs=(vmem,) * 4,
        scratch_shapes=[
            pltpu.VMEM((PIECES, 2, PROWS, HD), F32),
            pltpu.VMEM((GROUP, 2, PROWS, HD), F32),
            pltpu.VMEM((2, PROWS, HD), F32),
            pltpu.VMEM((2, REACH, PROWS, HD), F32),
            pltpu.VMEM((GROUP, 2, PROWS, HD), F32),
            pltpu.VMEM((PIECES, 2, PROWS, HD), F32),
            pltpu.VMEM((ROWS, HEADS * HD), BF16),
            pltpu.VMEM((4, ROWS, HEADS * HD), F32),
            dma((GROUP,)), dma((GROUP,)), dma((2, REACH)), dma((2, REACH)), dma((GROUP,)), dma((GROUP,)),
        ],
        compiler_params=pltpu.CompilerParams(
            collective_id=0, has_side_effects=True, vmem_limit_bytes=48 * 1024 * 1024),
        name="linear_attention",
    )(doc_lengths, query_rows, key_rows, value_rows, out_grad)


def solution(mesh):
    in_specs = (P("ctx", "head"), P("ctx", "head"), P("ctx", "head"), P("ctx", "head"), P("head"))
    out_specs = (P("ctx", "head"), P("ctx", "head"), P("ctx", "head"), P("ctx", "head"))
    return jax.shard_map(body, mesh=mesh, in_specs=in_specs, out_specs=out_specs, check_vma=False)
```

time: 342 us -> 52 us (0.15)
  the two profiles are of different devices: /device:TPU:30 before, /device:TPU:1 now
where the time goes in v1:
time: 52 us; the launch traced here: 51.7 us
  Pallas kernels  43.8 us (84%)
  local copies, waits for them, and re-layouts  7.26 us (14%)
  between operations  0.65 us (1%)
    pallas_call x1, Pallas kernels, body(): pl.pallas_call(kernel, out_shape=(out,) * 4, in_specs=[pl.BlockSpec(memor...  43.8 us
    unnamed x14, local copies, waits for them, and re-layouts  7.26 us

profile of v1, /device:TPU:1, one launch (start us, length us, event | category | flops | bytes accessed | tf_op | source)
XLA Modules:
  0.0 51.7 jit_solution(1698402191283839383)
XLA Ops:
  0.6 0.0 copy-start
  0.6 0.9 %copy-done = bf16[512,256]{1,0:T(8,128)(2,1)S(1)} copy-done((bf16[512,256]{1,0:T(8,128)(2,1)S(1)}, bf16[512,256]{1,0:T(8,128)(2,1)}, u32[]{:S(2)}) %copy-start) | copy-done | bytes 262168
  1.6 0.0 copy-start.1
  1.6 0.9 %copy-done.1 = bf16[512,256]{1,0:T(8,128)(2,1)S(1)} copy-done((bf16[512,256]{1,0:T(8,128)(2,1)S(1)}, bf16[512,256]{1,0:T(8,128)(2,1)}, u32[]{:S(2)}) %copy-start.1) | copy-done | bytes 262168
  2.5 0.0 copy-start.2
  2.5 0.9 %copy-done.2 = bf16[512,256]{1,0:T(8,128)(2,1)S(1)} copy-done((bf16[512,256]{1,0:T(8,128)(2,1)S(1)}, bf16[512,256]{1,0:T(8,128)(2,1)}, u32[]{:S(2)}) %copy-start.2) | copy-done | bytes 262168
  3.5 0.0 copy-start.3
  3.5 0.9 %copy-done.3 = bf16[512,256]{1,0:T(8,128)(2,1)S(1)} copy-done((bf16[512,256]{1,0:T(8,128)(2,1)S(1)}, bf16[512,256]{1,0:T(8,128)(2,1)}, u32[]{:S(2)}) %copy-start.3) | copy-done | bytes 262168
  4.4 0.0 copy-start.4
  4.4 0.7 %copy-done.4 = s32[8]{0:T(128)S(1)} copy-done((s32[8]{0:T(128)S(1)}, s32[8]{0:T(128)}, u32[]{:S(2)}) %copy-start.4) | copy-done | bytes 56
  5.1 43.8 %linear_attention.1 = (bf16[512,256]{1,0:T(8,128)(2,1)S(1)}, bf16[512,256]{1,0:T(8,128)(2,1)S(1)}, bf16[512,256]{1,0:T(8,128)(2,1)S(1)}, bf16[512,256]{1,0:T(8,128)(2,1)S(1)}) custom-call(s32[8]{0:T(128)S(1)} %copy-done.4, bf16[512,256]{1,0:T(8,128)(2,1)S(1)} %copy-done, bf16[512,256]{1,0:T(8,128)(2,1)S(1)} %copy-done.1, bf16[512,256]{1,0:T(8,128)(2,1)S(1)} %copy-done.2, ...), custom_call_target="tpu_custom_call" | custom-call | tf_op jit(solution)/shard_map/linear_attention/pallas_call | solution.py:242
  48.9 0.7 %copy.13 = bf16[512,256]{1,0:T(8,128)(2,1)} copy(bf16[512,256]{1,0:T(8,128)(2,1)S(1)} %get-tuple-element.8) | data formatting | bytes 524288
  49.6 0.7 %copy.14 = bf16[512,256]{1,0:T(8,128)(2,1)} copy(bf16[512,256]{1,0:T(8,128)(2,1)S(1)} %get-tuple-element.9) | data formatting | bytes 524288
  50.3 0.7 %copy.15 = bf16[512,256]{1,0:T(8,128)(2,1)} copy(bf16[512,256]{1,0:T(8,128)(2,1)S(1)} %get-tuple-element.10) | data formatting | bytes 524288
  51.0 0.7 %copy.16 = bf16[512,256]{1,0:T(8,128)(2,1)} copy(bf16[512,256]{1,0:T(8,128)(2,1)S(1)} %get-tuple-element.11) | data formatting | bytes 524288
Async XLA Ops:
  0.6 1.0 %copy-start = (bf16[512,256]{1,0:T(8,128)(2,1)S(1)}, bf16[512,256]{1,0:T(8,128)(2,1)}, u32[]{:S(2)}) copy-start(bf16[512,256]{1,0:T(8,128)(2,1)} %q_ref.1) | copy-start | bytes 786436
  1.6 0.9 %copy-start.1 = (bf16[512,256]{1,0:T(8,128)(2,1)S(1)}, bf16[512,256]{1,0:T(8,128)(2,1)}, u32[]{:S(2)}) copy-start(bf16[512,256]{1,0:T(8,128)(2,1)} %k_ref.1) | copy-start | bytes 786436
  2.5 0.9 %copy-start.2 = (bf16[512,256]{1,0:T(8,128)(2,1)S(1)}, bf16[512,256]{1,0:T(8,128)(2,1)}, u32[]{:S(2)}) copy-start(bf16[512,256]{1,0:T(8,128)(2,1)} %v_ref.1) | copy-start | bytes 786436
  3.5 0.9 %copy-start.3 = (bf16[512,256]{1,0:T(8,128)(2,1)S(1)}, bf16[512,256]{1,0:T(8,128)(2,1)}, u32[]{:S(2)}) copy-start(bf16[512,256]{1,0:T(8,128)(2,1)} %g_ref.1) | copy-start | bytes 786436
  4.4 0.7 %copy-start.4 = (s32[8]{0:T(128)S(1)}, s32[8]{0:T(128)}, u32[]{:S(2)}) copy-start(s32[8]{0:T(128)} %dl_ref.1) | copy-start | bytes 100

commit v2 on v1

v2 whole, which is shorter than its diff:
```python
import functools

import jax
import jax.numpy as jnp
from jax import lax
from jax.experimental import pallas as pl
from jax.experimental.pallas import tpu as pltpu
from jax.sharding import PartitionSpec as P

HD = 128
HEADS = 2
ROWS = 512
DOCS = 8
BLOCKS = 64
GROUP = 4
GROUPS = BLOCKS // GROUP
REACH = 4
GROUP_COLS = 4
COLUMNS = (2, 3, 1, 0)
PIECES = 4
PROWS = HEADS * HD // PIECES
MESH = pl.DeviceIdType.MESH
F32 = jnp.float32
BF16 = jnp.bfloat16
TN = (((0,), (0,)), ((), ()))
NT = (((1,), (1,)), ((), ()))
NN = (((1,), (0,)), ((), ()))


def dot(a, b, dims):
    return lax.dot_general(a, b, dims, preferred_element_type=F32)


def flag(cond):
    return jnp.where(cond, jnp.float32(1.0), jnp.float32(0.0))


def owner(group, piece):
    turned = (group % 4) // 2
    return piece + turned * (3 - 2 * piece)


def split(x):
    hi = x.astype(BF16)
    return hi, (x - hi.astype(F32)).astype(BF16)


def kernel(
    dl_hbm, q_hbm, k_hbm, v_hbm, g_hbm, att_ref, gq_ref, gk_ref, gv_ref,
    dl_ref, q_ref, k_ref, v_ref, g_ref,
    state, near_in, far_out, far_in, back_out, back_in, scaled_s, acc,
    ld, ss1, rs1, ss2, rs2, ss3, rs3,
):
    loads = [
        pltpu.make_async_copy(src, dst, ld.at[i])
        for i, (src, dst) in enumerate(
            [(dl_hbm, dl_ref), (k_hbm, k_ref), (v_hbm, v_ref), (q_hbm, q_ref), (g_hbm, g_ref)])
    ]
    for load in loads:
        load.start()

    c = lax.axis_index("ctx")
    h = lax.axis_index("head")
    grp = c // GROUP
    me = c % GROUP
    piece = owner(grp, me)

    def member(i):
        return (grp * GROUP + i, h)

    def far(step):
        other = (grp + step + GROUPS) % GROUPS
        return (other * GROUP + owner(other, piece), h)

    barrier = pltpu.get_barrier_semaphore()
    partners = [member((me + d) % GROUP) for d in range(1, GROUP)]
    partners += [far(s * d) for d in range(1, REACH + 1) for s in (1, -1)]
    for p in partners:
        pl.semaphore_signal(barrier, inc=1, device_id=p, device_id_type=MESH)

    loads[0].wait()
    starts, ends = [], []
    total = jnp.int32(0)
    for d in range(DOCS):
        starts.append(total)
        total = total + dl_ref[d]
        ends.append(total)

    def start_of(pos):
        best = jnp.int32(0)
        for d in range(1, DOCS):
            best = jnp.where(starts[d] <= pos, starts[d], best)
        return best

    def end_of(pos):
        best = ends[DOCS - 1]
        for d in range(DOCS - 2, -1, -1):
            best = jnp.where(ends[d] > pos, ends[d], best)
        return best

    base = c * ROWS
    last_start = start_of(base + ROWS - 1)
    first_end = end_of(base)
    pos = base + lax.broadcasted_iota(jnp.int32, (ROWS, HD), 0)
    doc_start = jnp.zeros((ROWS, HD), jnp.int32)
    for d in range(1, DOCS):
        doc_start = jnp.where(pos >= starts[d], starts[d], doc_start)
    row_scale = lax.rsqrt((pos - doc_start).astype(F32) + 1.0) * HD ** (-0.5)
    in_last = pos >= last_start
    in_first = pos < first_end

    def near_copy(scan, i, slot):
        return pltpu.make_async_remote_copy(
            state.at[scan, owner(grp, i)], near_in.at[scan, slot], ss1.at[scan, i], rs1.at[scan, slot],
            device_id=member(i), device_id_type=MESH)

    def near_send(scan):
        for d in (2, 3, 1):
            near_copy(scan, (me + d) % GROUP, me).start()
        near_in[scan, me] = state[scan, piece]

    def near_wait(scan):
        for d in (1, 2, 3):
            i = (me + d) % GROUP
            near_copy(scan, i, i).wait_recv()

    loads[1].wait()
    loads[2].wait()
    for hd in range(HEADS):
        cols = slice(hd * HD, (hd + 1) * HD)
        tail = jnp.where(in_last, k_ref[:, cols].astype(F32), 0.0).astype(BF16)
        st = dot(tail, v_ref[:, cols], TN)
        state[0, 2 * hd] = st[:PROWS]
        state[0, 2 * hd + 1] = st[PROWS:]
    pl.semaphore_wait(barrier, len(partners))
    near_send(0)

    loads[3].wait()
    loads[4].wait()
    for hd in range(HEADS):
        cols = slice(hd * HD, (hd + 1) * HD)
        sc = q_ref[:, cols].astype(F32) * row_scale
        scaled_s[:, cols] = sc.astype(BF16)
        head = jnp.where(in_first, sc, 0.0).astype(BF16)
        st = dot(head, g_ref[:, cols], TN)
        state[1, 2 * hd] = st[:PROWS]
        state[1, 2 * hd + 1] = st[PROWS:]
    near_send(1)

    def local_work(hd):
        cols = slice(hd * HD, (hd + 1) * HD)
        half = ROWS // 2
        for tb in range(2):
            rows = slice(tb * half, (tb + 1) * half)
            width = (tb + 1) * half
            sc, gr = scaled_s[rows, cols], g_ref[rows, cols]
            ke, va = k_ref[:width, cols], v_ref[:width, cols]
            col = base + lax.broadcasted_iota(jnp.int32, (half, width), 1)
            row = base + tb * half + lax.broadcasted_iota(jnp.int32, (half, width), 0)
            first = jnp.tile(doc_start[rows], (1, width // HD))
            allowed = (col <= row) & (col >= first)
            w = jnp.where(allowed, dot(sc, ke, NT), 0.0).astype(BF16)
            dw = jnp.where(allowed, dot(gr, va, NT), 0.0).astype(BF16)
            acc[0, rows, cols] = dot(w, va, NN)
            acc[1, rows, cols] = dot(dw, ke, NN)
            gk, gv = dot(dw, sc, TN), dot(w, gr, TN)
            if tb == 0:
                acc[2, rows, cols] = gk
                acc[3, rows, cols] = gv
            else:
                acc[2, :half, cols] += gk[:half]
                acc[3, :half, cols] += gv[:half]
                acc[2, half:, cols] = gk[half:]
                acc[3, half:, cols] = gv[half:]

    local_work(0)

    block0 = grp * GROUP
    gbase = block0 * ROWS
    gend = gbase + GROUP * ROWS
    col = grp % GROUP_COLS
    glast_start = start_of(gend - 1)
    gfirst_end = end_of(gbase)

    def far_copy(scan, d):
        return pltpu.make_async_remote_copy(
            far_out.at[scan], far_in.at[scan, d - 1], ss2.at[scan, d - 1], rs2.at[scan, d - 1],
            device_id=far(d if scan == 0 else -d), device_id_type=MESH)

    def far_send(scan, columns):
        for t in columns:
            step = t - col if scan == 0 else col - t
            far_copy(scan, (step + 2 * GROUP_COLS - 1) % GROUP_COLS + 1).start()

    near_wait(0)
    total = near_in[0, GROUP - 1]
    for i in range(GROUP - 1):
        total += flag(glast_start < gbase + (i + 1) * ROWS) * near_in[0, i]
    far_out[0] = total
    far_send(0, COLUMNS[:2])

    near_wait(1)
    total = near_in[1, 0]
    for i in range(1, GROUP):
        total += flag(gfirst_end > gbase + i * ROWS) * near_in[1, i]
    far_out[1] = total
    far_send(1, COLUMNS[:2])
    far_send(0, COLUMNS[2:])
    far_send(1, COLUMNS[2:])

    local_work(1)

    gfirst_start = start_of(gbase)
    glast_end = end_of(gend - 1)

    def back_copy(scan, i, slot):
        return pltpu.make_async_remote_copy(
            back_out.at[scan, i], back_in.at[scan, slot], ss3.at[scan, i], rs3.at[scan, slot],
            device_id=member(i), device_id_type=MESH)

    def back_send(scan):
        for d in (2, 3, 1):
            back_copy(scan, (me + d) % GROUP, piece).start()
        back_in[scan, piece] = back_out[scan, me]

    def back_wait(scan):
        for d in (1, 2, 3):
            i = (me + d) % GROUP
            back_copy(scan, i, owner(grp, i)).wait_recv()

    for d in range(1, REACH + 1):
        far_copy(0, d).wait_recv()
    outer = flag(gfirst_start < gbase) * far_in[0, 0]
    for d in range(2, REACH + 1):
        outer += flag(gfirst_start < gbase - (d - 1) * GROUP * ROWS) * far_in[0, d - 1]
    for i in range(GROUP):
        begin = start_of(gbase + i * ROWS)
        entering = flag(begin < gbase) * outer
        for r in range(i):
            entering += flag(begin < gbase + (r + 1) * ROWS) * near_in[0, r]
        back_out[0, i] = entering
    back_send(0)

    for d in range(1, REACH + 1):
        far_copy(1, d).wait_recv()
    outer = flag(glast_end > gend) * far_in[1, 0]
    for d in range(2, REACH + 1):
        outer += flag(glast_end > gbase + d * GROUP * ROWS) * far_in[1, d - 1]
    for i in range(GROUP):
        finish = end_of(gbase + (i + 1) * ROWS - 1)
        returning = flag(finish > gend) * outer
        for r in range(i + 1, GROUP):
            returning += flag(finish > gbase + r * ROWS) * near_in[1, r]
        back_out[1, i] = returning
    back_send(1)

    back_wait(0)
    for hd in range(HEADS):
        cols = slice(hd * HD, (hd + 1) * HD)
        e_hi, e_lo = split(jnp.concatenate([back_in[0, 2 * hd], back_in[0, 2 * hd + 1]], axis=0))
        sc, gr = scaled_s[:, cols], g_ref[:, cols]
        att = acc[0, :, cols] + dot(sc, e_hi, NN) + dot(sc, e_lo, NN)
        att_ref[:, cols] = att.astype(BF16)
        gq = acc[1, :, cols] + dot(gr, e_hi, NT) + dot(gr, e_lo, NT)
        gq_ref[:, cols] = (row_scale * gq).astype(BF16)
    back_wait(1)
    for hd in range(HEADS):
        cols = slice(hd * HD, (hd + 1) * HD)
        r_hi, r_lo = split(jnp.concatenate([back_in[1, 2 * hd], back_in[1, 2 * hd + 1]], axis=0))
        ke, va = k_ref[:, cols], v_ref[:, cols]
        gk = acc[2, :, cols] + dot(va, r_hi, NT) + dot(va, r_lo, NT)
        gk_ref[:, cols] = gk.astype(BF16)
        gv = acc[3, :, cols] + dot(ke, r_hi, NN) + dot(ke, r_lo, NN)
        gv_ref[:, cols] = gv.astype(BF16)

    for scan in range(2):
        for d in range(1, GROUP):
            i = (me + d) % GROUP
            near_copy(scan, i, i).wait_send()
            back_copy(scan, i, i).wait_send()
        for d in range(1, REACH + 1):
            far_copy(scan, d).wait_send()


def writer(*refs):
    srcs, dsts, sem = refs[:4], refs[4:8], refs[8]
    copies = [pltpu.make_async_copy(a, b, sem.at[i]) for i, (a, b) in enumerate(zip(srcs, dsts))]
    for copy in copies:
        copy.start()
    for copy in copies:
        copy.wait()


def body(query_rows, key_rows, value_rows, out_grad, doc_lengths):
    vmem = pl.BlockSpec(memory_space=pltpu.VMEM)
    out = jax.ShapeDtypeStruct((ROWS, HEADS * HD), BF16)
    dma = pltpu.SemaphoreType.DMA
    hbm = pl.BlockSpec(memory_space=pltpu.HBM)
    rows = pltpu.VMEM((ROWS, HEADS * HD), BF16)
    results = pl.pallas_call(
        kernel,
        out_shape=(pltpu.VMEM((ROWS, HEADS * HD), BF16),) * 4,
        in_specs=[hbm] * 5,
        out_specs=(vmem,) * 4,
        scratch_shapes=[
            pltpu.SMEM((DOCS,), jnp.int32), rows, rows, rows, rows,
            pltpu.VMEM((2, PIECES, PROWS, HD), F32),
            pltpu.VMEM((2, GROUP, PROWS, HD), F32),
            pltpu.VMEM((2, PROWS, HD), F32),
            pltpu.VMEM((2, REACH, PROWS, HD), F32),
            pltpu.VMEM((2, GROUP, PROWS, HD), F32),
            pltpu.VMEM((2, PIECES, PROWS, HD), F32),
            pltpu.VMEM((ROWS, HEADS * HD), BF16),
            pltpu.VMEM((4, ROWS, HEADS * HD), F32),
            dma((5,)), dma((2, GROUP)), dma((2, GROUP)), dma((2, REACH)), dma((2, REACH)),
            dma((2, GROUP)), dma((2, GROUP)),
        ],
        compiler_params=pltpu.CompilerParams(
            collective_id=0, has_side_effects=True),
        name="linear_attention",
    )(doc_lengths, query_rows, key_rows, value_rows, out_grad)
    return pl.pallas_call(
        writer,
        out_shape=(out,) * 4,
        in_specs=[vmem] * 4,
        out_specs=(hbm,) * 4,
        scratch_shapes=[dma((4,))],
        name="write_out",
    )(*[pltpu.with_memory_space_constraint(x, pltpu.VMEM) for x in results])


def solution(mesh):
    in_specs = (P("ctx", "head"), P("ctx", "head"), P("ctx", "head"), P("ctx", "head"), P("head"))
    out_specs = (P("ctx", "head"), P("ctx", "head"), P("ctx", "head"), P("ctx", "head"))
    return jax.shard_map(body, mesh=mesh, in_specs=in_specs, out_specs=out_specs, check_vma=False)
```

time: 52 us -> 43.8 us (0.84)
  the two profiles are of different devices: /device:TPU:1 before, /device:TPU:6 now
where the time goes in v2:
time: 43.8 us; the launch traced here: 43.7 us
  Pallas kernels  43 us (98%)
  between operations  0.64 us (1%)
    pallas_call x1, Pallas kernels, body(): pl.pallas_call(kernel, out_shape=(pltpu.VMEM((ROWS, HEADS * HD), BF16),)...  42 us
    pallas_call x1, Pallas kernels, body(): pl.pallas_call(writer, out_shape=(out,) * 4, in_specs=[vmem] * 4, out_spe...  1 us

profile of v2, /device:TPU:6, one launch (start us, length us, event | category | flops | bytes accessed | tf_op | source)
XLA Modules:
  0.0 43.7 jit_solution(15764570414960984572)
XLA Ops:
  0.6 42.0 %linear_attention.1 = (bf16[512,256]{1,0:T(8,128)(2,1)S(1)}, bf16[512,256]{1,0:T(8,128)(2,1)S(1)}, bf16[512,256]{1,0:T(8,128)(2,1)S(1)}, bf16[512,256]{1,0:T(8,128)(2,1)S(1)}) custom-call(s32[8]{0:T(128)} %dl_hbm.1, bf16[512,256]{1,0:T(8,128)(2,1)} %q_hbm.1, bf16[512,256]{1,0:T(8,128)(2,1)} %k_hbm.1, bf16[512,256]{1,0:T(8,128)(2,1)} %v_hbm.1, ...), custom_call_target="tpu_custom_call" | custom-call | tf_op jit(solution)/shard_map/linear_attention/pallas_call | solution.py:300
  42.7 1.0 %write_out.1 = (bf16[512,256]{1,0:T(8,128)(2,1)}, bf16[512,256]{1,0:T(8,128)(2,1)}, bf16[512,256]{1,0:T(8,128)(2,1)}, bf16[512,256]{1,0:T(8,128)(2,1)}) custom-call(bf16[512,256]{1,0:T(8,128)(2,1)S(1)} %get-tuple-element.8.refs_0_, bf16[512,256]{1,0:T(8,128)(2,1)S(1)} %get-tuple-element.9.refs_1_, bf16[512,256]{1,0:T(8,128)(2,1)S(1)} %get-tuple-element.10.refs_2_, ...), custom_call_target="tpu_custom_call" | custom-call | tf_op jit(solution)/shard_map/write_out/pallas_call | solution.py:322

commit v3 on v2

--- a/solution.py
+++ b/solution.py
@@ -16,7 +16,7 @@
 GROUPS = BLOCKS // GROUP
 REACH = 4
 GROUP_COLS = 4
-COLUMNS = (2, 3, 1, 0)
+FAR = [(scan, d) for d in range(1, REACH + 1) for scan in range(2)]
 PIECES = 4
 PROWS = HEADS * HD // PIECES
 MESH = pl.DeviceIdType.MESH
@@ -40,6 +40,12 @@
     return piece + turned * (3 - 2 * piece)
 
 
+def entry_order(group):
+    column = group % GROUP_COLS
+    place = column + (column // 2) * (5 - 2 * column)
+    return place * (GROUPS // GROUP_COLS) + group // GROUP_COLS
+
+
 def split(x):
     hi = x.astype(BF16)
     return hi, (x - hi.astype(F32)).astype(BF16)
@@ -49,7 +55,7 @@
     dl_hbm, q_hbm, k_hbm, v_hbm, g_hbm, att_ref, gq_ref, gk_ref, gv_ref,
     dl_ref, q_ref, k_ref, v_ref, g_ref,
     state, near_in, far_out, far_in, back_out, back_in, scaled_s, acc,
-    ld, ss1, rs1, ss2, rs2, ss3, rs3,
+    ld, ready, ss1, rs1, ss2, rs2, ss3, rs3,
 ):
     loads = [
         pltpu.make_async_copy(src, dst, ld.at[i])
@@ -72,11 +78,23 @@
         other = (grp + step + GROUPS) % GROUPS
         return (other * GROUP + owner(other, piece), h)
 
+    def after(step):
+        other = (grp + step + GROUPS) % GROUPS
+        return jnp.where(entry_order(other) > entry_order(grp), 1, 0)
+
+    later = [[after(d if scan == 0 else -d) for d in range(1, REACH + 1)] for scan in range(2)]
+
     barrier = pltpu.get_barrier_semaphore()
-    partners = [member((me + d) % GROUP) for d in range(1, GROUP)]
-    partners += [far(s * d) for d in range(1, REACH + 1) for s in (1, -1)]
-    for p in partners:
-        pl.semaphore_signal(barrier, inc=1, device_id=p, device_id_type=MESH)
+    awaited = jnp.int32(GROUP - 1)
+    for d in range(1, GROUP):
+        pl.semaphore_signal(barrier, inc=1, device_id=member((me + d) % GROUP), device_id_type=MESH)
+    for scan, d in FAR:
+        awaited = awaited + 1 - later[scan][d - 1]
+
+        @pl.when(later[scan][d - 1] == 1)
+        def _():
+            pl.semaphore_signal(
+                barrier, inc=1, device_id=far(d if scan == 0 else -d), device_id_type=MESH)
 
     loads[0].wait()
     starts, ends = [], []
@@ -132,8 +150,14 @@
         st = dot(tail, v_ref[:, cols], TN)
         state[0, 2 * hd] = st[:PROWS]
         state[0, 2 * hd + 1] = st[PROWS:]
-    pl.semaphore_wait(barrier, len(partners))
+    pl.semaphore_wait(barrier, awaited)
     near_send(0)
+    for scan, d in FAR:
+        @pl.when(later[scan][d - 1] == 0)
+        def _():
+            pl.semaphore_signal(
+                ready.at[1 - scan, d - 1], inc=1,
+                device_id=far(d if scan == 0 else -d), device_id_type=MESH)
 
     loads[3].wait()
     loads[4].wait()
@@ -178,7 +202,6 @@
     block0 = grp * GROUP
     gbase = block0 * ROWS
     gend = gbase + GROUP * ROWS
-    col = grp % GROUP_COLS
     glast_start = start_of(gend - 1)
     gfirst_end = end_of(gbase)
 
@@ -187,28 +210,32 @@
             far_out.at[scan], far_in.at[scan, d - 1], ss2.at[scan, d - 1], rs2.at[scan, d - 1],
             device_id=far(d if scan == 0 else -d), device_id_type=MESH)
 
-    def far_send(scan, columns):
-        for t in columns:
-            step = t - col if scan == 0 else col - t
-            far_copy(scan, (step + 2 * GROUP_COLS - 1) % GROUP_COLS + 1).start()
+    def far_send(scan, is_later):
+        for d in (2, 1, 3, 4):
+            @pl.when(later[scan][d - 1] == is_later)
+            def _():
+                if is_later:
+                    pl.semaphore_wait(ready.at[scan, d - 1], 1)
+                far_copy(scan, d).start()
 
     near_wait(0)
     total = near_in[0, GROUP - 1]
     for i in range(GROUP - 1):
         total += flag(glast_start < gbase + (i + 1) * ROWS) * near_in[0, i]
     far_out[0] = total
-    far_send(0, COLUMNS[:2])
+    far_send(0, 0)
 
     near_wait(1)
     total = near_in[1, 0]
     for i in range(1, GROUP):
         total += flag(gfirst_end > gbase + i * ROWS) * near_in[1, i]
     far_out[1] = total
-    far_send(1, COLUMNS[:2])
-    far_send(0, COLUMNS[2:])
-    far_send(1, COLUMNS[2:])
+    far_send(1, 0)
 
     local_work(1)
+
+    far_send(0, 1)
+    far_send(1, 1)
 
     gfirst_start = start_of(gbase)
     glast_end = end_of(gend - 1)
@@ -312,7 +339,7 @@
             pltpu.VMEM((2, PIECES, PROWS, HD), F32),
             pltpu.VMEM((ROWS, HEADS * HD), BF16),
             pltpu.VMEM((4, ROWS, HEADS * HD), F32),
-            dma((5,)), dma((2, GROUP)), dma((2, GROUP)), dma((2, REACH)), dma((2, REACH)),
+            dma((5,)), pltpu.SemaphoreType.REGULAR((2, REACH)), dma((2, GROUP)), dma((2, GROUP)), dma((2, REACH)), dma((2, REACH)),
             dma((2, GROUP)), dma((2, GROUP)),
         ],
         compiler_params=pltpu.CompilerParams(

time: 43.8 us -> 40.8 us (0.932)
  Pallas kernels: 43 us -> 39.9 us
    pallas_call x1, Pallas kernels: 42 us -> 38.9 us  [body(): pl.pallas_call(kernel, out_shape=(pltpu.VMEM((ROWS, HEADS * HD), BF16),)...]
where the time goes in v3:
time: 40.8 us; the launch traced here: 40.6 us
  Pallas kernels  39.9 us (98%)
  between operations  0.64 us (2%)
    pallas_call x1, Pallas kernels, body(): pl.pallas_call(kernel, out_shape=(pltpu.VMEM((ROWS, HEADS * HD), BF16),)...  38.9 us
    pallas_call x1, Pallas kernels, body(): pl.pallas_call(writer, out_shape=(out,) * 4, in_specs=[vmem] * 4, out_spe...  1 us

profile of v3, /device:TPU:6, one launch (start us, length us, event | category | flops | bytes accessed | tf_op | source)
XLA Modules:
  0.0 40.6 jit_solution(6865254439532986095)
XLA Ops:
  0.6 38.9 %linear_attention.1 = (bf16[512,256]{1,0:T(8,128)(2,1)S(1)}, bf16[512,256]{1,0:T(8,128)(2,1)S(1)}, bf16[512,256]{1,0:T(8,128)(2,1)S(1)}, bf16[512,256]{1,0:T(8,128)(2,1)S(1)}) custom-call(s32[8]{0:T(128)} %dl_hbm.1, bf16[512,256]{1,0:T(8,128)(2,1)} %q_hbm.1, bf16[512,256]{1,0:T(8,128)(2,1)} %k_hbm.1, bf16[512,256]{1,0:T(8,128)(2,1)} %v_hbm.1, ...), custom_call_target="tpu_custom_call" | custom-call | tf_op jit(solution)/shard_map/linear_attention/pallas_call | solution.py:327
  39.6 1.0 %write_out.1 = (bf16[512,256]{1,0:T(8,128)(2,1)}, bf16[512,256]{1,0:T(8,128)(2,1)}, bf16[512,256]{1,0:T(8,128)(2,1)}, bf16[512,256]{1,0:T(8,128)(2,1)}) custom-call(bf16[512,256]{1,0:T(8,128)(2,1)S(1)} %get-tuple-element.8.refs_0_, bf16[512,256]{1,0:T(8,128)(2,1)S(1)} %get-tuple-element.9.refs_1_, bf16[512,256]{1,0:T(8,128)(2,1)S(1)} %get-tuple-element.10.refs_2_, ...), custom_call_target="tpu_custom_call" | custom-call | tf_op jit(solution)/shard_map/write_out/pallas_call | solution.py:349

commit v4 on v3

--- a/solution.py
+++ b/solution.py
@@ -52,8 +52,9 @@
 
 
 def kernel(
-    dl_hbm, q_hbm, k_hbm, v_hbm, g_hbm, att_ref, gq_ref, gk_ref, gv_ref,
-    dl_ref, q_ref, k_ref, v_ref, g_ref,
+    dl_hbm, q_hbm, k_hbm, v_hbm, g_hbm,
+    att_ref, gq_ref, gk_acc, gv_acc, ret_ref, k_ref, v_ref,
+    dl_ref, q_ref, g_ref,
     state, near_in, far_out, far_in, back_out, back_in, scaled_s, acc,
     ld, ready, ss1, rs1, ss2, rs2, ss3, rs3,
 ):
@@ -79,17 +80,19 @@
         return (other * GROUP + owner(other, piece), h)
 
     def after(step):
-        other = (grp + step + GROUPS) % GROUPS
-        return jnp.where(entry_order(other) > entry_order(grp), 1, 0)
+        other = grp + step
+        turn = jnp.where(entry_order((other + GROUPS) % GROUPS) > entry_order(grp), 1, 0)
+        return jnp.where((other >= 0) & (other < GROUPS), turn, 2)
 
     later = [[after(d if scan == 0 else -d) for d in range(1, REACH + 1)] for scan in range(2)]
 
+    far_in[...] = jnp.zeros_like(far_in)
     barrier = pltpu.get_barrier_semaphore()
     awaited = jnp.int32(GROUP - 1)
     for d in range(1, GROUP):
         pl.semaphore_signal(barrier, inc=1, device_id=member((me + d) % GROUP), device_id_type=MESH)
     for scan, d in FAR:
-        awaited = awaited + 1 - later[scan][d - 1]
+        awaited = awaited + jnp.where(later[scan][d - 1] == 0, 1, 0)
 
         @pl.when(later[scan][d - 1] == 1)
         def _():
@@ -189,13 +192,13 @@
             acc[1, rows, cols] = dot(dw, ke, NN)
             gk, gv = dot(dw, sc, TN), dot(w, gr, TN)
             if tb == 0:
-                acc[2, rows, cols] = gk
-                acc[3, rows, cols] = gv
+                gk_acc[rows, cols] = gk
+                gv_acc[rows, cols] = gv
             else:
-                acc[2, :half, cols] += gk[:half]
-                acc[3, :half, cols] += gv[:half]
-                acc[2, half:, cols] = gk[half:]
-                acc[3, half:, cols] = gv[half:]
+                gk_acc[:half, cols] += gk[:half]
+                gv_acc[:half, cols] += gv[:half]
+                gk_acc[half:, cols] = gk[half:]
+                gv_acc[half:, cols] = gv[half:]
 
     local_work(0)
 
@@ -218,27 +221,51 @@
                     pl.semaphore_wait(ready.at[scan, d - 1], 1)
                 far_copy(scan, d).start()
 
+    def far_wait(scan):
+        for d in (4, 1, 3, 2):
+            @pl.when(later[1 - scan][d - 1] < 2)
+            def _():
+                far_copy(scan, d).wait_recv()
+
+    tail_on = [flag(glast_start < gbase + (i + 1) * ROWS) for i in range(GROUP - 1)]
+    head_on = [flag(gfirst_end > gbase + i * ROWS) for i in range(1, GROUP)]
     near_wait(0)
     total = near_in[0, GROUP - 1]
     for i in range(GROUP - 1):
-        total += flag(glast_start < gbase + (i + 1) * ROWS) * near_in[0, i]
+        total += tail_on[i] * near_in[0, i]
     far_out[0] = total
     far_send(0, 0)
 
     near_wait(1)
     total = near_in[1, 0]
     for i in range(1, GROUP):
-        total += flag(gfirst_end > gbase + i * ROWS) * near_in[1, i]
+        total += head_on[i - 1] * near_in[1, i]
     far_out[1] = total
     far_send(1, 0)
 
     local_work(1)
 
+    gfirst_start = start_of(gbase)
+    glast_end = end_of(gend - 1)
+    left_on = [flag(gfirst_start < gbase - (d - 1) * GROUP * ROWS) for d in range(1, REACH + 1)]
+    right_on = [flag(glast_end > gbase + d * GROUP * ROWS) for d in range(1, REACH + 1)]
+    open_left, open_right = [], []
+    for i in range(GROUP):
+        begin = start_of(gbase + i * ROWS)
+        finish = end_of(gbase + (i + 1) * ROWS - 1)
+        open_left.append(flag(begin < gbase))
+        open_right.append(flag(finish > gend))
+        inside = jnp.zeros((PROWS, HD), F32)
+        for r in range(i):
+            inside += flag(begin < gbase + (r + 1) * ROWS) * near_in[0, r]
+        back_out[0, i] = inside
+        inside = jnp.zeros((PROWS, HD), F32)
+        for r in range(i + 1, GROUP):
+            inside += flag(finish > gbase + r * ROWS) * near_in[1, r]
+        back_out[1, i] = inside
+
     far_send(0, 1)
     far_send(1, 1)
-
-    gfirst_start = start_of(gbase)
-    glast_end = end_of(gend - 1)
 
     def back_copy(scan, i, slot):
         return pltpu.make_async_remote_copy(
@@ -255,30 +282,20 @@
             i = (me + d) % GROUP
             back_copy(scan, i, owner(grp, i)).wait_recv()
 
-    for d in range(1, REACH + 1):
-        far_copy(0, d).wait_recv()
-    outer = flag(gfirst_start < gbase) * far_in[0, 0]
-    for d in range(2, REACH + 1):
-        outer += flag(gfirst_start < gbase - (d - 1) * GROUP * ROWS) * far_in[0, d - 1]
+    far_wait(0)
+    outer = left_on[0] * far_in[0, 0]
+    for d in range(1, REACH):
+        outer += left_on[d] * far_in[0, d]
     for i in range(GROUP):
-        begin = start_of(gbase + i * ROWS)
-        entering = flag(begin < gbase) * outer
-        for r in range(i):
-            entering += flag(begin < gbase + (r + 1) * ROWS) * near_in[0, r]
-        back_out[0, i] = entering
+        back_out[0, i] += open_left[i] * outer
     back_send(0)
 
-    for d in range(1, REACH + 1):
-        far_copy(1, d).wait_recv()
-    outer = flag(glast_end > gend) * far_in[1, 0]
-    for d in range(2, REACH + 1):
-        outer += flag(glast_end > gbase + d * GROUP * ROWS) * far_in[1, d - 1]
+    far_wait(1)
+    outer = right_on[0] * far_in[1, 0]
+    for d in range(1, REACH):
+        outer += right_on[d] * far_in[1, d]
     for i in range(GROUP):
-        finish = end_of(gbase + (i + 1) * ROWS - 1)
-        returning = flag(finish > gend) * outer
-        for r in range(i + 1, GROUP):
-            returning += flag(finish > gbase + r * ROWS) * near_in[1, r]
-        back_out[1, i] = returning
+        back_out[1, i] += open_right[i] * outer
     back_send(1)
 
     back_wait(0)
@@ -291,14 +308,7 @@
         gq = acc[1, :, cols] + dot(gr, e_hi, NT) + dot(gr, e_lo, NT)
         gq_ref[:, cols] = (row_scale * gq).astype(BF16)
     back_wait(1)
-    for hd in range(HEADS):
-        cols = slice(hd * HD, (hd + 1) * HD)
-        r_hi, r_lo = split(jnp.concatenate([back_in[1, 2 * hd], back_in[1, 2 * hd + 1]], axis=0))
-        ke, va = k_ref[:, cols], v_ref[:, cols]
-        gk = acc[2, :, cols] + dot(va, r_hi, NT) + dot(va, r_lo, NT)
-        gk_ref[:, cols] = gk.astype(BF16)
-        gv = acc[3, :, cols] + dot(ke, r_hi, NN) + dot(ke, r_lo, NN)
-        gv_ref[:, cols] = gv.astype(BF16)
+    ret_ref[...] = back_in[1]
 
     for scan in range(2):
         for d in range(1, GROUP):
@@ -306,14 +316,27 @@
             near_copy(scan, i, i).wait_send()
             back_copy(scan, i, i).wait_send()
         for d in range(1, REACH + 1):
-            far_copy(scan, d).wait_send()
-
-
-def writer(*refs):
-    srcs, dsts, sem = refs[:4], refs[4:8], refs[8]
-    copies = [pltpu.make_async_copy(a, b, sem.at[i]) for i, (a, b) in enumerate(zip(srcs, dsts))]
-    for copy in copies:
-        copy.start()
+            @pl.when(later[scan][d - 1] < 2)
+            def _():
+                far_copy(scan, d).wait_send()
+
+
+def writer(att_ref, gq_ref, gk_acc, gv_acc, ret_ref, k_ref, v_ref, *rest):
+    outs, gk_ref, gv_ref, sem = rest[:4], rest[4], rest[5], rest[6]
+    copies = [pltpu.make_async_copy(src, dst, sem.at[i]) for i, (src, dst) in enumerate(zip((att_ref, gq_ref, gk_ref, gv_ref), outs))]
+    copies[0].start()
+    copies[1].start()
+    r_all = [split(jnp.concatenate([ret_ref[2 * hd], ret_ref[2 * hd + 1]], axis=0)) for hd in range(HEADS)]
+    for hd in range(HEADS):
+        cols = slice(hd * HD, (hd + 1) * HD)
+        gk = gk_acc[:, cols] + dot(v_ref[:, cols], r_all[hd][0], NT) + dot(v_ref[:, cols], r_all[hd][1], NT)
+        gk_ref[:, cols] = gk.astype(BF16)
+    copies[2].start()
+    for hd in range(HEADS):
+        cols = slice(hd * HD, (hd + 1) * HD)
+        gv = gv_acc[:, cols] + dot(k_ref[:, cols], r_all[hd][0], NN) + dot(k_ref[:, cols], r_all[hd][1], NN)
+        gv_ref[:, cols] = gv.astype(BF16)
+    copies[3].start()
     for copy in copies:
         copy.wait()
 
@@ -324,13 +347,14 @@
     dma = pltpu.SemaphoreType.DMA
     hbm = pl.BlockSpec(memory_space=pltpu.HBM)
     rows = pltpu.VMEM((ROWS, HEADS * HD), BF16)
+    wide = pltpu.VMEM((ROWS, HEADS * HD), F32)
     results = pl.pallas_call(
         kernel,
-        out_shape=(pltpu.VMEM((ROWS, HEADS * HD), BF16),) * 4,
+        out_shape=(rows, rows, wide, wide, pltpu.VMEM((PIECES, PROWS, HD), F32), rows, rows),
         in_specs=[hbm] * 5,
-        out_specs=(vmem,) * 4,
+        out_specs=(vmem,) * 7,
         scratch_shapes=[
-            pltpu.SMEM((DOCS,), jnp.int32), rows, rows, rows, rows,
+            pltpu.SMEM((DOCS,), jnp.int32), rows, rows,
             pltpu.VMEM((2, PIECES, PROWS, HD), F32),
             pltpu.VMEM((2, GROUP, PROWS, HD), F32),
             pltpu.VMEM((2, PROWS, HD), F32),
@@ -338,7 +362,7 @@
             pltpu.VMEM((2, GROUP, PROWS, HD), F32),
             pltpu.VMEM((2, PIECES, PROWS, HD), F32),
             pltpu.VMEM((ROWS, HEADS * HD), BF16),
-            pltpu.VMEM((4, ROWS, HEADS * HD), F32),
+            pltpu.VMEM((2, ROWS, HEADS * HD), F32),
             dma((5,)), pltpu.SemaphoreType.REGULAR((2, REACH)), dma((2, GROUP)), dma((2, GROUP)), dma((2, REACH)), dma((2, REACH)),
             dma((2, GROUP)), dma((2, GROUP)),
         ],
@@ -349,9 +373,9 @@
     return pl.pallas_call(
         writer,
         out_shape=(out,) * 4,
-        in_specs=[vmem] * 4,
+        in_specs=[vmem] * 7,
         out_specs=(hbm,) * 4,
-        scratch_shapes=[dma((4,))],
+        scratch_shapes=[rows, rows, dma((4,))],
         name="write_out",
     )(*[pltpu.with_memory_space_constraint(x, pltpu.VMEM) for x in results])
 

time: 40.8 us -> 38.6 us (0.946)
  Pallas kernels: 39.9 us -> 37.8 us
    pallas_call x2, Pallas kernels: 39.9 us -> 37.8 us  [the longest x1 36.6 us: body(): pl.pallas_call(kernel, out_shape=(rows, rows, wide, wide, pltpu.VMEM((PIE...]
where the time goes in v4:
time: 38.6 us; the launch traced here: 38.5 us
  Pallas kernels  37.8 us (98%)
  between operations  0.64 us (2%)
    pallas_call x1, Pallas kernels, body(): pl.pallas_call(kernel, out_shape=(rows, rows, wide, wide, pltpu.VMEM((PIE...  36.6 us
    pallas_call x1, Pallas kernels, body(): pl.pallas_call(writer, out_shape=(out,) * 4, in_specs=[vmem] * 7, out_spe...  1.18 us

profile of v4, /device:TPU:6, one launch (start us, length us, event | category | flops | bytes accessed | tf_op | source)
XLA Modules:
  0.0 38.5 jit_solution(2856858552114422639)
XLA Ops:
  0.6 36.6 %linear_attention.1 = (bf16[512,256]{1,0:T(8,128)(2,1)S(1)}, bf16[512,256]{1,0:T(8,128)(2,1)S(1)}, f32[512,256]{1,0:T(8,128)S(1)}, f32[512,256]{1,0:T(8,128)S(1)...) custom-call(s32[8]{0:T(128)} %dl_hbm.1, bf16[512,256]{1,0:T(8,128)(2,1)} %q_hbm.1, ...), custom_call_target="tpu_custom_call" | custom-call | tf_op jit(solution)/shard_map/linear_attention/pallas_call | solution.py:351
  37.3 1.2 %write_out.1 = (bf16[512,256]{1,0:T(8,128)(2,1)}, bf16[512,256]{1,0:T(8,128)(2,1)}, bf16[512,256]{1,0:T(8,128)(2,1)}, bf16[512,256]{1,0:T(8,128)(2,1)}) custom-call(bf16[512,256]{1,0:T(8,128)(2,1)S(1)} %get-tuple-element.11.att_ref, bf16[512,256]{1,0:T(8,128)(2,1)S(1)} %get-tuple-element.12.gq_ref, f32[512,256]{1,0:T(8,128)S(1)} %get-tuple-element.13.gk_acc, ...), custom_call_target="tpu_custom_call" | custom-call | tf_op jit(solution)/shard_map/write_out/pallas_call | solution.py:373

commit v5 on v4

--- a/solution.py
+++ b/solution.py
@@ -136,8 +136,10 @@
             device_id=member(i), device_id_type=MESH)
 
     def near_send(scan):
-        for d in (2, 3, 1):
-            near_copy(scan, (me + d) % GROUP, me).start()
+        for i in (1, 2, 0, 3):
+            @pl.when(me != i)
+            def _():
+                near_copy(scan, i, me).start()
         near_in[scan, me] = state[scan, piece]
 
     def near_wait(scan):
@@ -205,6 +207,7 @@
     block0 = grp * GROUP
     gbase = block0 * ROWS
     gend = gbase + GROUP * ROWS
+    col = grp % GROUP_COLS
     glast_start = start_of(gend - 1)
     gfirst_end = end_of(gbase)
 
@@ -213,13 +216,26 @@
             far_out.at[scan], far_in.at[scan, d - 1], ss2.at[scan, d - 1], rs2.at[scan, d - 1],
             device_id=far(d if scan == 0 else -d), device_id_type=MESH)
 
-    def far_send(scan, is_later):
-        for d in (2, 1, 3, 4):
-            @pl.when(later[scan][d - 1] == is_later)
-            def _():
-                if is_later:
-                    pl.semaphore_wait(ready.at[scan, d - 1], 1)
-                far_copy(scan, d).start()
+    def far_send(scan, column):
+        step = column - col if scan == 0 else col - column
+        d = (step + 2 * GROUP_COLS - 1) % GROUP_COLS + 1
+        turn = after(d if scan == 0 else -d)
+
+        @pl.when(turn == 1)
+        def _():
+            pl.semaphore_wait(ready.at[scan, d - 1], 1)
+
+        @pl.when(turn < 2)
+        def _():
+            far_copy(scan, d).start()
+
+    def far_sent(scan, column):
+        step = column - col if scan == 0 else col - column
+        d = (step + 2 * GROUP_COLS - 1) % GROUP_COLS + 1
+
+        @pl.when(after(d if scan == 0 else -d) < 2)
+        def _():
+            far_copy(scan, d).wait_send()
 
     def far_wait(scan):
         for d in (4, 1, 3, 2):
@@ -244,6 +260,10 @@
     far_send(1, 0)
 
     local_work(1)
+    far_sent(0, 0)
+    far_sent(1, 0)
+    far_send(0, 1)
+    far_send(1, 1)
 
     gfirst_start = start_of(gbase)
     glast_end = end_of(gend - 1)
@@ -264,8 +284,11 @@
             inside += flag(finish > gbase + r * ROWS) * near_in[1, r]
         back_out[1, i] = inside
 
-    far_send(0, 1)
-    far_send(1, 1)
+    far_sent(0, 1)
+    far_sent(1, 1)
+    for column in (2, 3):
+        far_send(0, column)
+        far_send(1, column)
 
     def back_copy(scan, i, slot):
         return pltpu.make_async_remote_copy(
@@ -273,8 +296,10 @@
             device_id=member(i), device_id_type=MESH)
 
     def back_send(scan):
-        for d in (2, 3, 1):
-            back_copy(scan, (me + d) % GROUP, piece).start()
+        for i in range(GROUP):
+            @pl.when(me != i)
+            def _():
+                back_copy(scan, i, piece).start()
         back_in[scan, piece] = back_out[scan, me]
 
     def back_wait(scan):
@@ -315,10 +340,8 @@
             i = (me + d) % GROUP
             near_copy(scan, i, i).wait_send()
             back_copy(scan, i, i).wait_send()
-        for d in range(1, REACH + 1):
-            @pl.when(later[scan][d - 1] < 2)
-            def _():
-                far_copy(scan, d).wait_send()
+        for column in (2, 3):
+            far_sent(scan, column)
 
 
 def writer(att_ref, gq_ref, gk_acc, gv_acc, ret_ref, k_ref, v_ref, *rest):

time: 38.6 us -> 36.7 us (0.951)
  the two profiles are of different devices: /device:TPU:6 before, /device:TPU:136 now
where the time goes in v5:
time: 36.7 us; the launch traced here: 36.6 us
  Pallas kernels  35.9 us (98%)
  between operations  0.64 us (2%)
    pallas_call x1, Pallas kernels, body(): pl.pallas_call(kernel, out_shape=(rows, rows, wide, wide, pltpu.VMEM((PIE...  34.8 us
    pallas_call x1, Pallas kernels, body(): pl.pallas_call(writer, out_shape=(out,) * 4, in_specs=[vmem] * 7, out_spe...  1.18 us

profile of v5, /device:TPU:136, one launch (start us, length us, event | category | flops | bytes accessed | tf_op | source)
XLA Modules:
  0.0 36.6 jit_solution(13002296156008431226)
XLA Ops:
  0.6 34.8 %linear_attention.1 = (bf16[512,256]{1,0:T(8,128)(2,1)S(1)}, bf16[512,256]{1,0:T(8,128)(2,1)S(1)}, f32[512,256]{1,0:T(8,128)S(1)}, f32[512,256]{1,0:T(8,128)S(1)...) custom-call(s32[8]{0:T(128)} %dl_hbm.1, bf16[512,256]{1,0:T(8,128)(2,1)} %q_hbm.1, ...), custom_call_target="tpu_custom_call" | custom-call | tf_op jit(solution)/shard_map/linear_attention/pallas_call | solution.py:374
  35.4 1.2 %write_out.1 = (bf16[512,256]{1,0:T(8,128)(2,1)}, bf16[512,256]{1,0:T(8,128)(2,1)}, bf16[512,256]{1,0:T(8,128)(2,1)}, bf16[512,256]{1,0:T(8,128)(2,1)}) custom-call(bf16[512,256]{1,0:T(8,128)(2,1)S(1)} %get-tuple-element.11.att_ref, bf16[512,256]{1,0:T(8,128)(2,1)S(1)} %get-tuple-element.12.gq_ref, f32[512,256]{1,0:T(8,128)S(1)} %get-tuple-element.13.gk_acc, ...), custom_call_target="tpu_custom_call" | custom-call | tf_op jit(solution)/shard_map/write_out/pallas_call | solution.py:396

commit v6 on v5

--- a/solution.py
+++ b/solution.py
@@ -286,9 +286,9 @@
 
     far_sent(0, 1)
     far_sent(1, 1)
-    for column in (2, 3):
-        far_send(0, column)
-        far_send(1, column)
+    for scan in range(2):
+        for column in (2, 3):
+            far_send(scan, column)
 
     def back_copy(scan, i, slot):
         return pltpu.make_async_remote_copy(
@@ -332,9 +332,6 @@
         att_ref[:, cols] = att.astype(BF16)
         gq = acc[1, :, cols] + dot(gr, e_hi, NT) + dot(gr, e_lo, NT)
         gq_ref[:, cols] = (row_scale * gq).astype(BF16)
-    back_wait(1)
-    ret_ref[...] = back_in[1]
-
     for scan in range(2):
         for d in range(1, GROUP):
             i = (me + d) % GROUP
@@ -342,6 +339,9 @@
             back_copy(scan, i, i).wait_send()
         for column in (2, 3):
             far_sent(scan, column)
+
+    back_wait(1)
+    ret_ref[...] = back_in[1]
 
 
 def writer(att_ref, gq_ref, gk_acc, gv_acc, ret_ref, k_ref, v_ref, *rest):

time: 36.7 us -> 36.3 us (0.989)
  the two profiles are of different devices: /device:TPU:136 before, /device:TPU:150 now
where the time goes in v6:
time: 36.3 us; the launch traced here: 36.2 us
  Pallas kernels  35.5 us (98%)
  between operations  0.64 us (2%)
    pallas_call x1, Pallas kernels, body(): pl.pallas_call(kernel, out_shape=(rows, rows, wide, wide, pltpu.VMEM((PIE...  34.4 us
    pallas_call x1, Pallas kernels, body(): pl.pallas_call(writer, out_shape=(out,) * 4, in_specs=[vmem] * 7, out_spe...  1.18 us

profile of v6, /device:TPU:150, one launch (start us, length us, event | category | flops | bytes accessed | tf_op | source)
XLA Modules:
  0.0 36.2 jit_solution(2287924824208107478)
XLA Ops:
  0.6 34.4 %linear_attention.1 = (bf16[512,256]{1,0:T(8,128)(2,1)S(1)}, bf16[512,256]{1,0:T(8,128)(2,1)S(1)}, f32[512,256]{1,0:T(8,128)S(1)}, f32[512,256]{1,0:T(8,128)S(1)...) custom-call(s32[8]{0:T(128)} %dl_hbm.1, bf16[512,256]{1,0:T(8,128)(2,1)} %q_hbm.1, ...), custom_call_target="tpu_custom_call" | custom-call | tf_op jit(solution)/shard_map/linear_attention/pallas_call | solution.py:374
  35.0 1.2 %write_out.1 = (bf16[512,256]{1,0:T(8,128)(2,1)}, bf16[512,256]{1,0:T(8,128)(2,1)}, bf16[512,256]{1,0:T(8,128)(2,1)}, bf16[512,256]{1,0:T(8,128)(2,1)}) custom-call(bf16[512,256]{1,0:T(8,128)(2,1)S(1)} %get-tuple-element.11.att_ref, bf16[512,256]{1,0:T(8,128)(2,1)S(1)} %get-tuple-element.12.gq_ref, f32[512,256]{1,0:T(8,128)S(1)} %get-tuple-element.13.gk_acc, ...), custom_call_target="tpu_custom_call" | custom-call | tf_op jit(solution)/shard_map/write_out/pallas_call | solution.py:396

commit v7 on v6

--- a/solution.py
+++ b/solution.py
@@ -123,12 +123,7 @@
     last_start = start_of(base + ROWS - 1)
     first_end = end_of(base)
     pos = base + lax.broadcasted_iota(jnp.int32, (ROWS, HD), 0)
-    doc_start = jnp.zeros((ROWS, HD), jnp.int32)
-    for d in range(1, DOCS):
-        doc_start = jnp.where(pos >= starts[d], starts[d], doc_start)
-    row_scale = lax.rsqrt((pos - doc_start).astype(F32) + 1.0) * HD ** (-0.5)
     in_last = pos >= last_start
-    in_first = pos < first_end
 
     def near_copy(scan, i, slot):
         return pltpu.make_async_remote_copy(
@@ -157,13 +152,11 @@
         state[0, 2 * hd + 1] = st[PROWS:]
     pl.semaphore_wait(barrier, awaited)
     near_send(0)
-    for scan, d in FAR:
-        @pl.when(later[scan][d - 1] == 0)
-        def _():
-            pl.semaphore_signal(
-                ready.at[1 - scan, d - 1], inc=1,
-                device_id=far(d if scan == 0 else -d), device_id_type=MESH)
-
+    doc_start = jnp.zeros((ROWS, HD), jnp.int32)
+    for d in range(1, DOCS):
+        doc_start = jnp.where(pos >= starts[d], starts[d], doc_start)
+    row_scale = lax.rsqrt((pos - doc_start).astype(F32) + 1.0) * HD ** (-0.5)
+    in_first = pos < first_end
     loads[3].wait()
     loads[4].wait()
     for hd in range(HEADS):
@@ -175,6 +168,12 @@
         state[1, 2 * hd] = st[:PROWS]
         state[1, 2 * hd + 1] = st[PROWS:]
     near_send(1)
+    for scan, d in FAR:
+        @pl.when(later[scan][d - 1] == 0)
+        def _():
+            pl.semaphore_signal(
+                ready.at[1 - scan, d - 1], inc=1,
+                device_id=far(d if scan == 0 else -d), device_id_type=MESH)
 
     def local_work(hd):
         cols = slice(hd * HD, (hd + 1) * HD)

time: 36.3 us -> 36 us (level)
  the two profiles are of different devices: /device:TPU:150 before, /device:TPU:142 now
where the time goes in v7:
time: 36 us; the launch traced here: 35.9 us
  Pallas kernels  35.2 us (98%)
  between operations  0.64 us (2%)
    pallas_call x1, Pallas kernels, body(): pl.pallas_call(kernel, out_shape=(rows, rows, wide, wide, pltpu.VMEM((PIE...  34 us
    pallas_call x1, Pallas kernels, body(): pl.pallas_call(writer, out_shape=(out,) * 4, in_specs=[vmem] * 7, out_spe...  1.18 us

profile of v7, /device:TPU:142, one launch (start us, length us, event | category | flops | bytes accessed | tf_op | source)
XLA Modules:
  0.0 35.9 jit_solution(12206638633455674525)
XLA Ops:
  0.6 34.0 %linear_attention.1 = (bf16[512,256]{1,0:T(8,128)(2,1)S(1)}, bf16[512,256]{1,0:T(8,128)(2,1)S(1)}, f32[512,256]{1,0:T(8,128)S(1)}, f32[512,256]{1,0:T(8,128)S(1)...) custom-call(s32[8]{0:T(128)} %dl_hbm.1, bf16[512,256]{1,0:T(8,128)(2,1)} %q_hbm.1, ...), custom_call_target="tpu_custom_call" | custom-call | tf_op jit(solution)/shard_map/linear_attention/pallas_call | solution.py:373
  34.7 1.2 %write_out.1 = (bf16[512,256]{1,0:T(8,128)(2,1)}, bf16[512,256]{1,0:T(8,128)(2,1)}, bf16[512,256]{1,0:T(8,128)(2,1)}, bf16[512,256]{1,0:T(8,128)(2,1)}) custom-call(bf16[512,256]{1,0:T(8,128)(2,1)S(1)} %get-tuple-element.11.att_ref, bf16[512,256]{1,0:T(8,128)(2,1)S(1)} %get-tuple-element.12.gq_ref, f32[512,256]{1,0:T(8,128)S(1)} %get-tuple-element.13.gk_acc, ...), custom_call_target="tpu_custom_call" | custom-call | tf_op jit(solution)/shard_map/write_out/pallas_call | solution.py:395

commit v8 on v7

--- a/solution.py
+++ b/solution.py
@@ -86,11 +86,11 @@
 
     later = [[after(d if scan == 0 else -d) for d in range(1, REACH + 1)] for scan in range(2)]
 
-    far_in[...] = jnp.zeros_like(far_in)
     barrier = pltpu.get_barrier_semaphore()
-    awaited = jnp.int32(GROUP - 1)
     for d in range(1, GROUP):
         pl.semaphore_signal(barrier, inc=1, device_id=member((me + d) % GROUP), device_id_type=MESH)
+    far_in[...] = jnp.zeros_like(far_in)
+    awaited = jnp.int32(GROUP - 1)
     for scan, d in FAR:
         awaited = awaited + jnp.where(later[scan][d - 1] == 0, 1, 0)
 

time: 36 us -> 36 us (level)
  the two profiles are of different devices: /device:TPU:142 before, /device:TPU:140 now
where the time goes in v8:
time: 36 us; the launch traced here: 35.9 us
  Pallas kernels  35.2 us (98%)
  between operations  0.64 us (2%)
    pallas_call x1, Pallas kernels, body(): pl.pallas_call(kernel, out_shape=(rows, rows, wide, wide, pltpu.VMEM((PIE...  34.1 us
    pallas_call x1, Pallas kernels, body(): pl.pallas_call(writer, out_shape=(out,) * 4, in_specs=[vmem] * 7, out_spe...  1.18 us

profile of v8, /device:TPU:140, one launch (start us, length us, event | category | flops | bytes accessed | tf_op | source)
XLA Modules:
  0.0 35.9 jit_solution(816375670009552318)
XLA Ops:
  0.6 34.1 %linear_attention.1 = (bf16[512,256]{1,0:T(8,128)(2,1)S(1)}, bf16[512,256]{1,0:T(8,128)(2,1)S(1)}, f32[512,256]{1,0:T(8,128)S(1)}, f32[512,256]{1,0:T(8,128)S(1)...) custom-call(s32[8]{0:T(128)} %dl_hbm.1, bf16[512,256]{1,0:T(8,128)(2,1)} %q_hbm.1, ...), custom_call_target="tpu_custom_call" | custom-call | tf_op jit(solution)/shard_map/linear_attention/pallas_call | solution.py:373
  34.7 1.2 %write_out.1 = (bf16[512,256]{1,0:T(8,128)(2,1)}, bf16[512,256]{1,0:T(8,128)(2,1)}, bf16[512,256]{1,0:T(8,128)(2,1)}, bf16[512,256]{1,0:T(8,128)(2,1)}) custom-call(bf16[512,256]{1,0:T(8,128)(2,1)S(1)} %get-tuple-element.11.att_ref, bf16[512,256]{1,0:T(8,128)(2,1)S(1)} %get-tuple-element.12.gq_ref, f32[512,256]{1,0:T(8,128)S(1)} %get-tuple-element.13.gk_acc, ...), custom_call_target="tpu_custom_call" | custom-call | tf_op jit(solution)/shard_map/write_out/pallas_call | solution.py:395
